TPU v7x, 256 devices: a whole 4x4x8 slice. The times are simulated.
256 devices in a mesh: mem: 4 (over y), tile: 32 (over x, z_hi, core), grp: 2 (over z_lo).
Axes of the slice: x: 4, y: 4, z: 8 (z_hi: 4, z_lo: 2; z = z_hi * 2 + z_lo), core: 2. Of those that a mesh axis runs over, the one named last changes fastest.
Arguments:
- members: float32 [3, 128, 512, 512], P(None, 'mem', ('tile', 'grp')), may hold values from -0.6 to 0.6
- obs_cells: int32 [64, 4, 1024], P(('tile', 'grp'), 'mem'), may hold values from 0 to 1023
- obs_count: int32 [64, 4], P(('tile', 'grp'), 'mem'), may hold values from 128 to 1024, as said below
- obs_values: float32 [64, 4, 1024], P(('tile', 'grp'), 'mem'), may hold values from -0.6 to 0.6
- obs_error: float32 [64, 4, 1024], P(('tile', 'grp'), 'mem'), may hold values from 0.03 to 0.3
- obs_noise: float32 [64, 4, 1024, 128], P(('tile', 'grp'), 'mem'), may hold values from -6 to 6
Outputs:
- analysis: bfloat16 [3, 128, 512, 512], P(None, None, ('tile', 'grp'), 'mem')
Inputs may be any that keep to these rules, and one draw needn't show every extreme that they name: `obs_count`: a multiple of 128; some tile has exactly 1024 live slots in every draw.
All inputs are finite; a program needn't handle non-finite values.
Results may differ from a plain program's by a relative error of at most 0.0058.
Values may be sent and summed in bfloat16 or wider, within the bound.
No kernel may reach another device: no remote copies, remote signals or barrier semaphores. Data moves between devices by JAX's collectives and lax.ppermute only.
A program may use at most 64 MiB of HBM per device.

v0:
```python
import functools

import jax
import jax.numpy as jnp
from jax import lax
from jax.experimental import pallas as pl
from jax.experimental.pallas import tpu as pltpu
from jax.sharding import PartitionSpec as P

STEPS = 4
F32 = jnp.float32
BF16 = jnp.bfloat16
HIGHEST = lax.Precision.HIGHEST
CH = 0.09
CU = 0.3
MIB = 1 << 20


def dot(a, b):
    return jnp.dot(a, b, preferred_element_type=F32, precision=HIGHEST)


def dot_t(a, b, precision=HIGHEST):
    return lax.dot_general(
        a, b, (((1,), (1,)), ((), ())), preferred_element_type=F32, precision=precision
    )


def edges_kernel(x_ref, low_ref, high_ref):
    members, cols = low_ref.shape[2:]
    for f in range(3):
        for r in range(STEPS):
            for t in range(cols // 128):
                part = pl.ds(t * 128, 128)
                for out_ref, row in ((low_ref, r), (high_ref, 8 - STEPS + r)):
                    q = x_ref[f, pl.ds(t * 8 + row, members, stride=cols // 16), :]
                    out_ref[f, r, :, part] = q.astype(BF16)


def edges(x, cols):
    members = x.shape[1] * 16 // cols
    half = members // 2
    shape = jax.ShapeDtypeStruct((3, STEPS, members, cols), BF16)
    return pl.pallas_call(
        edges_kernel,
        grid=(2,),
        in_specs=[pl.BlockSpec((3, half * cols // 16, 128), lambda i: (0, i, 0))],
        out_specs=[pl.BlockSpec((3, STEPS, half, cols), lambda i: (0, 0, i, 0))] * 2,
        out_shape=[shape, shape],
        compiler_params=pltpu.CompilerParams(vmem_limit_bytes=32 * MIB),
        cost_estimate=pl.CostEstimate(flops=x.size, bytes_accessed=x.size * 6, transcendentals=0),
        name="edges",
    )(x)


def forecast_kernel(x_ref, below_ref, above_ref, h_ref, uv_ref, ping, pong, edge):
    members, cols = below_ref.shape[2], below_ref.shape[3]
    tiles = h_ref.shape[0]
    stride = cols // 16
    for f in range(3):
        for r in range(STEPS):
            edge[f, r] = below_ref[f, r].astype(F32)
            edge[f, STEPS + r] = above_ref[f, r].astype(F32)

    def north(q):
        return pltpu.roll(q, cols - 1, axis=1)

    def south(q):
        return pltpu.roll(q, 1, axis=1)

    def group(g, _):
        first = pl.multiple_of(g * 8, 8)

        def start(f, p):
            if p < STEPS:
                q = edge[f, p, pl.ds(first, 8), :]
            elif p < STEPS + 8:
                base = pl.multiple_of(g * (8 * stride), 8 * stride) + (p - STEPS)
                q = jnp.concatenate(
                    [x_ref[f, pl.ds(base + t * 8, 8, stride=stride), :] for t in range(tiles)], axis=1
                )
            else:
                q = edge[f, p - 8, pl.ds(first, 8), :]
            return q * CH + CH if f == 0 else q * CU

        for step in range(STEPS):
            source, target = (ping, pong) if step % 2 else (pong, ping)

            def row(p):
                if step == 0:
                    h, u, v = (start(f, p) for f in range(3))
                else:
                    h, u, v = (source[f, p, pl.ds(first, 8), :] for f in range(3))
                up, um = 0.25 + u, 0.25 - u
                flux = 0.5 * (u * u) + h
                quarter = 0.25 * u
                return dict(
                    h=h, u=u, v=v, up=up, um=um,
                    he=h * um, hw=h * up, ue=quarter - flux, uw=quarter + flux,
                )

            west, mid = row(step), row(step + 1)
            for p in range(step + 1, 15 - step):
                east = row(p + 1)
                h, u, v = mid["h"], mid["u"], mid["v"]
                vp, vm = 0.25 + v, 0.25 - v
                flux = 0.5 * (v * v) + h
                quarter = 0.25 * v
                new_h = (east["he"] + west["hw"]) + (north(h * vm) + south(h * vp))
                new_u = (east["ue"] + west["uw"]) + (north(u) * vm + south(u) * vp) + 0.1 * v
                new_v = (
                    (north(quarter - flux) + south(quarter + flux))
                    + (east["v"] * mid["um"] + west["v"] * mid["up"])
                    - 0.1 * u
                )
                for f, q in enumerate((new_h, new_u, new_v)):
                    target[f, p, pl.ds(first, 8), :] = q
                west, mid = mid, east
        return 0

    lax.fori_loop(0, members // 8, group, 0)
    last = pong if STEPS % 2 == 0 else ping
    for r in range(8):
        for t in range(tiles):
            part = pl.ds(t * 128, 128)
            h_ref[t, r] = (last[0, STEPS + r, :, part] * (1.0 / CH) - 1.0).astype(BF16)
            for f in range(2):
                uv_ref[t, f, r] = (last[1 + f, STEPS + r, :, part] * (1.0 / CU)).astype(BF16)


def forecast(x, below, above, tiles):
    members, cols = below.shape[2:]
    half = members // 2
    edge_spec = pl.BlockSpec((3, STEPS, half, cols), lambda i: (0, 0, i, 0))
    return pl.pallas_call(
        forecast_kernel,
        grid=(2,),
        in_specs=[
            pl.BlockSpec((3, half * cols // 16, 128), lambda i: (0, i, 0)),
            edge_spec,
            edge_spec,
        ],
        out_specs=[
            pl.BlockSpec((tiles, 8, half, 128), lambda i: (0, 0, i, 0)),
            pl.BlockSpec((tiles, 2, 8, half, 128), lambda i: (0, 0, 0, i, 0)),
        ],
        out_shape=[
            jax.ShapeDtypeStruct((tiles, 8, members, 128), BF16),
            jax.ShapeDtypeStruct((tiles, 2, 8, members, 128), BF16),
        ],
        scratch_shapes=[
            pltpu.VMEM((3, 16, half, cols), F32),
            pltpu.VMEM((3, 16, half, cols), F32),
            pltpu.VMEM((3, 2 * STEPS, half, cols), F32),
        ],
        compiler_params=pltpu.CompilerParams(vmem_limit_bytes=40 * MIB),
        cost_estimate=pl.CostEstimate(flops=x.size * 200, bytes_accessed=x.size * 8, transcendentals=0),
        name="forecast",
    )(x, below, above)


def slots_kernel(count_ref, cells_ref, values_ref, error_ref, noise_ref, z_ref, omega_ref, lhs):
    slots = cells_ref.shape[1]
    members = noise_ref.shape[1]
    error = error_ref[...]
    live = lax.broadcasted_iota(jnp.int32, (1, slots), 1) < count_ref[0, 0]
    weight = jnp.where(live, 1.0 / (error * error), 0.0)
    rows = members + 16

    def put(at, size, cols, value):
        high = value.astype(BF16)
        rest = value - high.astype(F32)
        middle = rest.astype(BF16)
        low = (rest - middle.astype(F32)).astype(BF16)
        for k, q in enumerate((high, middle, low)):
            lhs[pl.ds(k * rows + at, size), cols] = q

    for b in range(slots // 128):
        part = pl.ds(b * 128, 128)
        lane = slice(b * 128, (b + 1) * 128)
        innovation = values_ref[:, part] + error[:, lane] * noise_ref[part, :].T
        put(0, members, part, weight[:, lane] * innovation)
    put(members, 16, pl.ds(0, slots), jnp.broadcast_to(weight, (16, slots)))
    block = 256
    cells = cells_ref[...]
    for b in range(z_ref.shape[1] // block):
        ids = lax.broadcasted_iota(jnp.int32, (block, slots), 0) + b * block
        chosen = jnp.where(ids == cells, 1.0, 0.0).astype(BF16)
        total = lax.dot_general(
            lhs[...], chosen, (((1,), (1,)), ((), ())), preferred_element_type=F32
        )
        total = total[:rows] + (total[rows : 2 * rows] + total[2 * rows :])
        part = pl.ds(b * block, block)
        z_ref[:, part] = total[:members]
        omega_ref[:, part] = total[members : members + 8]


def slots_to_cells(count, cells, values, error, noise):
    slots, members = noise.shape
    vmem = pl.BlockSpec(memory_space=pltpu.VMEM)
    return pl.pallas_call(
        slots_kernel,
        in_specs=[pl.BlockSpec(memory_space=pltpu.SMEM)] + [vmem] * 4,
        out_specs=[vmem, vmem],
        out_shape=[
            jax.ShapeDtypeStruct((members, 1024), F32),
            jax.ShapeDtypeStruct((8, 1024), F32),
        ],
        scratch_shapes=[pltpu.VMEM((3 * (members + 16), slots), BF16)],
        compiler_params=pltpu.CompilerParams(vmem_limit_bytes=32 * MIB),
        cost_estimate=pl.CostEstimate(
            flops=4 * members * slots * 1024, bytes_accessed=8 * noise.size, transcendentals=0
        ),
        name="slots_to_cells",
    )(count, cells, values, error, noise)


def weights_kernel(rank_ref, z_ref, omega_ref, p0, p1, p2, p3, w_ref, x_ref, lhs, t_ref, q_ref):
    parts = (p0, p1, p2, p3)
    size = p0.shape[1]
    members = size * len(parts)
    for s, part in enumerate(parts):
        for r in range(8):
            x_ref[pl.ds(s * size, size), pl.ds(r * 128, 128)] = part[r].astype(F32)
    x = x_ref[...]
    mean = jnp.sum(x, axis=0, keepdims=True) * (1.0 / members)
    x = x - mean
    omega = omega_ref[pl.ds(0, 1), :]
    lhs[pl.ds(0, members), :] = x * omega
    lhs[pl.ds(members, members), :] = z_ref[...] - omega * mean
    both = dot_t(lhs[...], x)
    shape = (members, members)
    down = lax.broadcasted_iota(jnp.int32, shape, 0)
    across = lax.broadcasted_iota(jnp.int32, shape, 1)
    eye = jnp.where(down == across, 1.0, 0.0)
    source = rank_ref[0, 0] + len(parts) - across // size
    source = jnp.where(source >= len(parts), source - len(parts), source)
    own = jnp.where(down == source * size + across % size, 1.0, 0.0)
    diagonal = members - 1.0
    gram = both[:members]
    rhs = both[members:] + diagonal * own
    square = dot(gram, gram)
    gram = gram + diagonal * eye
    top = jnp.sqrt(jnp.sqrt(jnp.sum(square * square)))
    low = 0.98 * diagonal
    high = 1.01 * (diagonal + top)
    inv = 1.0 / (high - low)
    z = (high + low) * inv
    alpha = (high + low - 2.0 * diagonal) * inv
    beta = 2.0 * inv
    less = gram - diagonal * eye
    t1 = alpha * eye - beta * less
    t2 = (2.0 * alpha * alpha - 1.0) * eye - (4.0 * alpha * beta) * less + (2.0 * beta * beta) * square
    z2 = 2.0 * z * z - 1.0
    t_ref[...] = t2
    q_ref[...] = (2.0 / (high + low)) * (2.0 * z / z2) * (z * eye + t1)

    def double(t):
        cheb, q = t_ref[...], q_ref[...]
        after = 2.0 * t * t - 1.0
        q_ref[...] = (2.0 * t / after) * (t * q + dot(q, cheb))
        t_ref[...] = 2.0 * dot(cheb, cheb) - eye
        return after

    lax.while_loop(lambda t: t < 3000.0, double, z2)
    inverse = q_ref[...]
    w = dot(rhs, inverse)
    w = w + dot(rhs - dot(w, gram), inverse)
    high_part = w.astype(BF16)
    w_ref[:, pl.ds(0, members)] = high_part
    w_ref[:, pl.ds(members, members)] = (w - high_part.astype(F32)).astype(BF16)


def weights(rank, z, omega, parts):
    members = z.shape[0]
    vmem = pl.BlockSpec(memory_space=pltpu.VMEM)
    return pl.pallas_call(
        weights_kernel,
        in_specs=[pl.BlockSpec(memory_space=pltpu.SMEM)] + [vmem] * 6,
        out_specs=vmem,
        out_shape=jax.ShapeDtypeStruct((members, 2 * members), BF16),
        scratch_shapes=[
            pltpu.VMEM((members, 1024), F32),
            pltpu.VMEM((2 * members, 1024), F32),
            pltpu.VMEM((members, members), F32),
            pltpu.VMEM((members, members), F32),
        ],
        compiler_params=pltpu.CompilerParams(vmem_limit_bytes=32 * MIB),
        cost_estimate=pl.CostEstimate(
            flops=100 * members**3, bytes_accessed=8 * z.size, transcendentals=0
        ),
        name="weights",
    )(rank, z, omega, *parts)


def apply_kernel(w_ref, *refs):
    h_parts, uv_parts, out_ref, stage = refs[:4], refs[4:8], refs[8], refs[9]
    members = out_ref.shape[1] // 8
    w = w_ref[...]
    for f in range(3):
        for r in range(8):
            pieces = [p[r] for p in h_parts] if f == 0 else [p[f - 1, r] for p in uv_parts]
            x = jnp.concatenate(pieces + pieces, axis=0)
            stage[pl.ds(r, members, stride=8), :] = jnp.dot(w, x, preferred_element_type=F32)
        out_ref[f] = stage[...].astype(BF16)


def apply_weights(w, h_parts, uv_parts):
    members = w.shape[0]
    vmem = pl.BlockSpec(memory_space=pltpu.VMEM)
    return pl.pallas_call(
        apply_kernel,
        in_specs=[vmem] * 9,
        out_specs=vmem,
        out_shape=jax.ShapeDtypeStruct((3, members * 8, 128), BF16),
        scratch_shapes=[pltpu.VMEM((members * 8, 128), F32)],
        compiler_params=pltpu.CompilerParams(vmem_limit_bytes=32 * MIB),
        cost_estimate=pl.CostEstimate(
            flops=12 * members * members * 1024, bytes_accessed=12 * members * 1024, transcendentals=0
        ),
        name="apply_weights",
    )(w, *h_parts, *uv_parts)


def send(x, axis, shift):
    size = lax.axis_size(axis)
    return lax.ppermute(x, axis, [(i, (i + shift) % size) for i in range(size)])


def body(members, obs_cells, obs_count, obs_values, obs_error, obs_noise):
    rows = ("tile", "grp")
    fields, count, lines, cols = members.shape
    x = members.reshape(fields, count, lines, cols // 128, 128)
    x = x.transpose(0, 1, 3, 2, 4).reshape(fields, -1, 128)
    low, high = edges(x, cols)
    below = send(high, rows, 1)
    above = send(low, rows, -1)
    slots = obs_cells.shape[-1]
    z, omega = slots_to_cells(
        obs_count,
        obs_cells.reshape(1, slots),
        obs_values.reshape(1, slots),
        obs_error.reshape(1, slots),
        obs_noise.reshape(slots, -1),
    )
    size = lax.axis_size("mem")
    h, uv = forecast(x, below, above, size)
    rank = lax.axis_index("mem")

    def exchange(blocks):
        parts = []
        for shift in range(size):
            block = lax.dynamic_index_in_dim(blocks, (rank + shift) % size, 0, keepdims=False)
            parts.append(send(block, "mem", shift) if shift else block)
        return parts

    h_parts = exchange(h)
    uv_parts = exchange(uv)
    w = weights(rank.astype(jnp.int32).reshape(1, 1), z, omega, h_parts)
    out = apply_weights(w, h_parts, uv_parts)
    return out.reshape(fields, -1, lines, 128)


def solution(mesh):
    in_specs = (
        P(None, "mem", ("tile", "grp"), None),
        P(("tile", "grp"), "mem", None),
        P(("tile", "grp"), "mem"),
        P(("tile", "grp"), "mem", None),
        P(("tile", "grp"), "mem", None),
        P(("tile", "grp"), "mem", None, None),
    )
    out_specs = P(None, None, ("tile", "grp"), "mem")
    return jax.shard_map(body, mesh=mesh, in_specs=in_specs, out_specs=out_specs, check_vma=False)
```

profile of v0, /device:TPU:8, one launch (start us, length us, event | category | flops | bytes accessed | tf_op | source)
XLA Modules:
  0.0 42.4 jit_solution(1272401875499719867)
XLA Ops:
  0.0 0.0 copy-start
  0.0 1.4 %copy-done = f32[3,32,8,512]{3,2,1,0:T(8,128)S(1)} copy-done((f32[3,32,8,512]{3,2,1,0:T(8,128)S(1)}, f32[3,32,8,512]{3,2,1,0:T(8,128)}, u32[]{:S(2)}) %copy-start) | copy-done | bytes 1572888
  1.4 0.0 copy-start.1
  1.4 1.1 %edges.1 = (bf16[3,4,32,512]{3,2,1,0:T(8,128)(2,1)S(1)}, bf16[3,4,32,512]{3,2,1,0:T(8,128)(2,1)S(1)}) custom-call(f32[3,1024,128]{2,1,0:T(8,128)S(1)} %bitcast.27), custom_call_target="tpu_custom_call" | custom-call | flops 393216 | bytes 2359296 | tf_op jit(solution)/shard_map/edges/pallas_call | solution.py:44
  2.5 2.0 %collective-permute-start = (bf16[3,4,32,512]{3,2,1,0:T(8,128)(2,1)S(1)}, bf16[3,4,32,512]{3,2,1,0:T(8,128)(2,1)S(1)}, u32[]{:S(2)}, u32[]{:S(2)}) collective-permute-start(bf16[3,4,32,512]{3,2,1,0:T(8,128)(2,1)S(1)} %get-tuple-element.13), channel_id=1, source_target_pairs={{0,1},{1,2},{2,3},{3,4},{4,5},{5,6},{6,7},{7,8},{8,9},{9,10},{10,1... | collective-permute-start | bytes 1179656 | tf_op jit(solution)/shard_map/ppermute | solution.py:327
  4.5 5.7 %collective-permute-start.1 = (bf16[3,4,32,512]{3,2,1,0:T(8,128)(2,1)S(1)}, bf16[3,4,32,512]{3,2,1,0:T(8,128)(2,1)S(1)}, u32[]{:S(2)}, u32[]{:S(2)}) collective-permute-start(bf16[3,4,32,512]{3,2,1,0:T(8,128)(2,1)S(1)} %get-tuple-element.14), channel_id=1, source_target_pairs={{0,63},{1,0},{2,1},{3,2},{4,3},{5,4},{6,5},{7,6},{8,7},{9,8},{10,9... | collective-permute-start | bytes 1179656 | tf_op jit(solution)/shard_map/ppermute | solution.py:327
  10.2 0.0 copy-start.2
  10.2 0.0 copy-start.3
  10.2 0.0 copy-start.4
  10.2 0.0 copy-start.5
  10.2 5.4 %collective-permute-done.below_ref = bf16[3,4,32,512]{3,2,1,0:T(8,128)(2,1)S(1)} collective-permute-done((bf16[3,4,32,512]{3,2,1,0:T(8,128)(2,1)S(1)}, bf16[3,4,32,512]{3,2,1,0:T(8,128)(2,1)S(1)}, u32[]{:S(2)}, u32[]{:S(2)}) %collective-permute-start) | collective-permute-done | bytes 393248 | tf_op jit(solution)/shard_map/ppermute | solution.py:327
  15.6 3.1 %collective-permute-done.1.above_ref = bf16[3,4,32,512]{3,2,1,0:T(8,128)(2,1)S(1)} collective-permute-done((bf16[3,4,32,512]{3,2,1,0:T(8,128)(2,1)S(1)}, bf16[3,4,32,512]{3,2,1,0:T(8,128)(2,1)S(1)}, u32[]{:S(2)}, u32[]{:S(2)}) %collective-permute-start.1) | collective-permute-done | bytes 393248 | tf_op jit(solution)/shard_map/ppermute | solution.py:327
  18.7 0.0 copy-done.1
  18.7 6.0 %forecast.1 = (bf16[4,8,32,128]{3,2,1,0:T(8,128)(2,1)S(1)}, bf16[4,2,8,32,128]{4,3,2,1,0:T(8,128)(2,1)S(1)}) custom-call(f32[3,1024,128]{2,1,0:T(8,128)S(1)} %bitcast.28, bf16[3,4,32,512]{3,2,1,0:T(8,128)(2,1)S(1)} %collective-permute-done.below_ref, bf16[3,4,32,512]{3,2,1,0:T(8,128)(2,1)S(1)} %collective-permute-done.1.above_ref), custom_call_target="tpu_custom_call" | custom-call | flops 78643200 | bytes 3145728 | tf_op jit(solution)/shard_map/forecast/pallas_call | solution.py:135
  24.8 1.7 %collective-permute-start.2 = (bf16[8,32,128]{2,1,0:T(8,128)(2,1)S(1)}, bf16[8,32,128]{2,1,0:T(8,128)(2,1)S(1)}, u32[]{:S(2)}, u32[]{:S(2)}) collective-permute-start(bf16[8,32,128]{2,1,0:T(8,128)(2,1)S(1)} %get-tuple-element.23), channel_id=1, source_target_pairs={{0,64},{64,128},{128,192},{192,0},{1,65},{65,129},{129,193},{193,1... | collective-permute-start | bytes 196616 | tf_op jit(solution)/shard_map/ppermute | solution.py:327
  26.5 1.4 %collective-permute-start.5 = (bf16[2,8,32,128]{3,2,1,0:T(8,128)(2,1)S(1)}, bf16[2,8,32,128]{3,2,1,0:T(8,128)(2,1)S(1)}, u32[]{:S(2)}, u32[]{:S(2)}) collective-permute-start(bf16[2,8,32,128]{3,2,1,0:T(8,128)(2,1)S(1)} %get-tuple-element.19), channel_id=1, source_target_pairs={{0,64},{64,128},{128,192},{192,0},{1,65},{65,129},{129,193},{193,1... | collective-permute-start | bytes 393224 | tf_op jit(solution)/shard_map/ppermute | solution.py:327
  27.8 1.2 %collective-permute-start.6 = (bf16[2,8,32,128]{3,2,1,0:T(8,128)(2,1)S(1)}, bf16[2,8,32,128]{3,2,1,0:T(8,128)(2,1)S(1)}, u32[]{:S(2)}, u32[]{:S(2)}) collective-permute-start(bf16[2,8,32,128]{3,2,1,0:T(8,128)(2,1)S(1)} %get-tuple-element.18), channel_id=1, source_target_pairs={{0,128},{64,192},{128,0},{192,64},{1,129},{65,193},{129,1},{193,65... | collective-permute-start | bytes 393224 | tf_op jit(solution)/shard_map/ppermute | solution.py:327
  29.1 1.1 %collective-permute-start.7 = (bf16[2,8,32,128]{3,2,1,0:T(8,128)(2,1)S(1)}, bf16[2,8,32,128]{3,2,1,0:T(8,128)(2,1)S(1)}, u32[]{:S(2)}, u32[]{:S(2)}) collective-permute-start(bf16[2,8,32,128]{3,2,1,0:T(8,128)(2,1)S(1)} %get-tuple-element.17), channel_id=1, source_target_pairs={{0,192},{64,0},{128,64},{192,128},{1,193},{65,1},{129,65},{193,129... | collective-permute-start | bytes 393224 | tf_op jit(solution)/shard_map/ppermute | solution.py:327
  30.1 1.4 %collective-permute-start.3 = (bf16[8,32,128]{2,1,0:T(8,128)(2,1)S(1)}, bf16[8,32,128]{2,1,0:T(8,128)(2,1)S(1)}, u32[]{:S(2)}, u32[]{:S(2)}) collective-permute-start(bf16[8,32,128]{2,1,0:T(8,128)(2,1)S(1)} %get-tuple-element.22), channel_id=1, source_target_pairs={{0,128},{64,192},{128,0},{192,64},{1,129},{65,193},{129,1},{193,65... | collective-permute-start | bytes 196616 | tf_op jit(solution)/shard_map/ppermute | solution.py:327
  31.5 0.0 collective-permute-done.2.p1.refs_1_
  31.5 1.7 %collective-permute-start.4 = (bf16[8,32,128]{2,1,0:T(8,128)(2,1)S(1)}, bf16[8,32,128]{2,1,0:T(8,128)(2,1)S(1)}, u32[]{:S(2)}, u32[]{:S(2)}) collective-permute-start(bf16[8,32,128]{2,1,0:T(8,128)(2,1)S(1)} %get-tuple-element.21), channel_id=1, source_target_pairs={{0,192},{64,0},{128,64},{192,128},{1,193},{65,1},{129,65},{193,129... | collective-permute-start | bytes 196616 | tf_op jit(solution)/shard_map/ppermute | solution.py:327
  33.8 0.0 copy-done.2
  33.8 0.0 copy-done.3
  33.8 0.0 copy-done.4
  33.8 0.0 copy-done.5
  33.9 1.2 %slots_to_cells.1 = (f32[128,1024]{1,0:T(8,128)S(1)}, f32[8,1024]{1,0:T(8,128)S(1)}) custom-call(s32[1,1]{1,0:T(1,128)S(6)} %copy.7.count_ref, s32[1,1024]{1,0:T(1,128)S(1)} %bitcast.30, f32[1,1024]{1,0:T(1,128)S(1)} %bitcast.31, f32[1,1024]{1,0:T(1,128)S(1)} %bitcast.32, f32[1024,128]{1,0:T(8,128)S(1)} %bitcast.29), custom_call_target="tpu_custom_call" | custom-call | flops 536870912 | bytes 1048576 | tf_op jit(solution)/shard_map/slots_to_cells/pallas_call | solution.py:201
  35.0 2.7 %collective-permute-done.3.p2.refs_2_ = bf16[8,32,128]{2,1,0:T(8,128)(2,1)S(1)} collective-permute-done((bf16[8,32,128]{2,1,0:T(8,128)(2,1)S(1)}, bf16[8,32,128]{2,1,0:T(8,128)(2,1)S(1)}, u32[]{:S(2)}, u32[]{:S(2)}) %collective-permute-start.3) | collective-permute-done | bytes 65568 | tf_op jit(solution)/shard_map/ppermute | solution.py:327
  37.8 0.0 collective-permute-done.4.p3.refs_3_
  37.8 3.1 %weights.1.w_ref = bf16[128,256]{1,0:T(8,128)(2,1)S(1)} custom-call(s32[1,1]{1,0:T(1,128)} %bitcast.rank_ref, f32[128,1024]{1,0:T(8,128)S(1)} %get-tuple-element.11.z_ref, f32[8,1024]{1,0:T(8,128)S(1)} %get-tuple-element.12.omega_ref, bf16[8,32,128]{2,1,0:T(8,128)(2,1)S(1)} %get-tuple-element.24.p0.refs_0_, ...), custom_call_target="tpu_custom_call" | custom-call | flops 209715200 | bytes 1048576 | tf_op jit(solution)/shard_map/weights/pallas_call | solution.py:277
  40.9 0.0 collective-permute-done.5.refs_5_
  40.9 0.0 collective-permute-done.6.refs_6_
  40.9 0.0 collective-permute-done.7.refs_7_
  40.9 1.5 %apply_weights.1 = bf16[3,1024,128]{2,1,0:T(8,128)(2,1)} custom-call(bf16[128,256]{1,0:T(8,128)(2,1)S(1)} %weights.1.w_ref, bf16[8,32,128]{2,1,0:T(8,128)(2,1)S(1)} %get-tuple-element.24.p0.refs_0_, bf16[8,32,128]{2,1,0:T(8,128)(2,1)S(1)} %collective-permute-done.2.p1.refs_1_, bf16[8,32,128]{2,1,0:T(8,128)(2,1)S(1)} %collective-permute-done.3.p2.refs_2_, ...), custom_call_target="tpu_custom_call" | custom-call | flops 201326592 | bytes 1572864 | tf_op jit(solution)/shard_map/apply_weights/pallas_call | solution.py:311
  (2 shorter events, 0.1 us)
Async XLA Ops:
  0.0 1.4 %copy-start = (f32[3,32,8,512]{3,2,1,0:T(8,128)S(1)}, f32[3,32,8,512]{3,2,1,0:T(8,128)}, u32[]{:S(2)}) copy-start(f32[3,32,8,512]{3,2,1,0:T(8,128)} %param.6) | copy-start | bytes 4718596
  1.4 17.3 %copy-start.1 = (f32[3,32,8,512]{3,2,1,0:T(8,128)S(1)}, f32[3,32,8,512]{3,2,1,0:T(8,128)}, u32[]{:S(2)}) copy-start(f32[3,32,8,512]{3,2,1,0:T(8,128)} %param.6) | copy-start | bytes 4718596
  2.5 13.0 %collective-permute-start = (bf16[3,4,32,512]{3,2,1,0:T(8,128)(2,1)S(1)}, bf16[3,4,32,512]{3,2,1,0:T(8,128)(2,1)S(1)}, u32[]{:S(2)}, u32[]{:S(2)}) collective-permute-start(bf16[3,4,32,512]{3,2,1,0:T(8,128)(2,1)S(1)} %get-tuple-element.13), channel_id=1, source_target_pairs={{0,1},{1,2},{2,3},{3,4},{4,5},{5,6},{6,7},{7,8},{8,9},{9,10},{10,1... | collective-permute-start | bytes 1179656 | tf_op jit(solution)/shard_map/ppermute | solution.py:327
  4.5 14.2 %collective-permute-start.1 = (bf16[3,4,32,512]{3,2,1,0:T(8,128)(2,1)S(1)}, bf16[3,4,32,512]{3,2,1,0:T(8,128)(2,1)S(1)}, u32[]{:S(2)}, u32[]{:S(2)}) collective-permute-start(bf16[3,4,32,512]{3,2,1,0:T(8,128)(2,1)S(1)} %get-tuple-element.14), channel_id=1, source_target_pairs={{0,63},{1,0},{2,1},{3,2},{4,3},{5,4},{6,5},{7,6},{8,7},{9,8},{10,9... | collective-permute-start | bytes 1179656 | tf_op jit(solution)/shard_map/ppermute | solution.py:327
  10.2 23.6 %copy-start.2 = (f32[1,1,1024,128]{3,2,1,0:T(8,128)S(1)}, f32[1,1,1024,128]{3,2,1,0:T(8,128)}, u32[]{:S(2)}) copy-start(f32[1,1,1024,128]{3,2,1,0:T(8,128)} %param.11) | copy-start | bytes 1572868
  10.2 23.6 %copy-start.3 = (s32[1,1,1024]{2,1,0:T(1,128)S(1)}, s32[1,1,1024]{2,1,0:T(1,128)}, u32[]{:S(2)}) copy-start(s32[1,1,1024]{2,1,0:T(1,128)} %param.7) | copy-start | bytes 12292
  10.2 23.6 %copy-start.4 = (f32[1,1,1024]{2,1,0:T(1,128)S(1)}, f32[1,1,1024]{2,1,0:T(1,128)}, u32[]{:S(2)}) copy-start(f32[1,1,1024]{2,1,0:T(1,128)} %param.9) | copy-start | bytes 12292
  10.2 23.6 %copy-start.5 = (f32[1,1,1024]{2,1,0:T(1,128)S(1)}, f32[1,1,1024]{2,1,0:T(1,128)}, u32[]{:S(2)}) copy-start(f32[1,1,1024]{2,1,0:T(1,128)} %param.10) | copy-start | bytes 12292
  24.8 6.7 %collective-permute-start.2 = (bf16[8,32,128]{2,1,0:T(8,128)(2,1)S(1)}, bf16[8,32,128]{2,1,0:T(8,128)(2,1)S(1)}, u32[]{:S(2)}, u32[]{:S(2)}) collective-permute-start(bf16[8,32,128]{2,1,0:T(8,128)(2,1)S(1)} %get-tuple-element.23), channel_id=1, source_target_pairs={{0,64},{64,128},{128,192},{192,0},{1,65},{65,129},{129,193},{193,1... | collective-permute-start | bytes 196616 | tf_op jit(solution)/shard_map/ppermute | solution.py:327
  26.5 14.4 %collective-permute-start.5 = (bf16[2,8,32,128]{3,2,1,0:T(8,128)(2,1)S(1)}, bf16[2,8,32,128]{3,2,1,0:T(8,128)(2,1)S(1)}, u32[]{:S(2)}, u32[]{:S(2)}) collective-permute-start(bf16[2,8,32,128]{3,2,1,0:T(8,128)(2,1)S(1)} %get-tuple-element.19), channel_id=1, source_target_pairs={{0,64},{64,128},{128,192},{192,0},{1,65},{65,129},{129,193},{193,1... | collective-permute-start | bytes 393224 | tf_op jit(solution)/shard_map/ppermute | solution.py:327
  27.8 13.0 %collective-permute-start.6 = (bf16[2,8,32,128]{3,2,1,0:T(8,128)(2,1)S(1)}, bf16[2,8,32,128]{3,2,1,0:T(8,128)(2,1)S(1)}, u32[]{:S(2)}, u32[]{:S(2)}) collective-permute-start(bf16[2,8,32,128]{3,2,1,0:T(8,128)(2,1)S(1)} %get-tuple-element.18), channel_id=1, source_target_pairs={{0,128},{64,192},{128,0},{192,64},{1,129},{65,193},{129,1},{193,65... | collective-permute-start | bytes 393224 | tf_op jit(solution)/shard_map/ppermute | solution.py:327
  29.1 11.8 %collective-permute-start.7 = (bf16[2,8,32,128]{3,2,1,0:T(8,128)(2,1)S(1)}, bf16[2,8,32,128]{3,2,1,0:T(8,128)(2,1)S(1)}, u32[]{:S(2)}, u32[]{:S(2)}) collective-permute-start(bf16[2,8,32,128]{3,2,1,0:T(8,128)(2,1)S(1)} %get-tuple-element.17), channel_id=1, source_target_pairs={{0,192},{64,0},{128,64},{192,128},{1,193},{65,1},{129,65},{193,129... | collective-permute-start | bytes 393224 | tf_op jit(solution)/shard_map/ppermute | solution.py:327
  30.1 7.6 %collective-permute-start.3 = (bf16[8,32,128]{2,1,0:T(8,128)(2,1)S(1)}, bf16[8,32,128]{2,1,0:T(8,128)(2,1)S(1)}, u32[]{:S(2)}, u32[]{:S(2)}) collective-permute-start(bf16[8,32,128]{2,1,0:T(8,128)(2,1)S(1)} %get-tuple-element.22), channel_id=1, source_target_pairs={{0,128},{64,192},{128,0},{192,64},{1,129},{65,193},{129,1},{193,65... | collective-permute-start | bytes 196616 | tf_op jit(solution)/shard_map/ppermute | solution.py:327
  31.5 6.3 %collective-permute-start.4 = (bf16[8,32,128]{2,1,0:T(8,128)(2,1)S(1)}, bf16[8,32,128]{2,1,0:T(8,128)(2,1)S(1)}, u32[]{:S(2)}, u32[]{:S(2)}) collective-permute-start(bf16[8,32,128]{2,1,0:T(8,128)(2,1)S(1)} %get-tuple-element.21), channel_id=1, source_target_pairs={{0,192},{64,0},{128,64},{192,128},{1,193},{65,1},{129,65},{193,129... | collective-permute-start | bytes 196616 | tf_op jit(solution)/shard_map/ppermute | solution.py:327
where the time goes:
time: 42.9 us; the launch traced here: 42.4 us
  starting transfers between devices  16 us (37%)
  Pallas kernels  12.9 us (30%)
  waiting for transfers between devices  11.3 us (26%)
  local copies, waits for them, and re-layouts  1.49 us (3%)
  between operations  0.76 us (2%)
    ppermute x8, starting transfers between devices, send(): return lax.ppermute(x, axis, [(i, (i + shift) % size) for i in range(size)])  16 us
    ppermute x8, waiting for transfers between devices, send(): return lax.ppermute(x, axis, [(i, (i + shift) % size) for i in range(size)])  11.3 us
    pallas_call x1, Pallas kernels, forecast(): pl.pallas_call(forecast_kernel, grid=(2,), in_specs=[pl.BlockSpec((3, hal...  6.01 us
    pallas_call x1, Pallas kernels, weights(): pl.pallas_call(weights_kernel, in_specs=[pl.BlockSpec(memory_space=pltpu....  3.09 us
    pallas_call x1, Pallas kernels, apply_weights(): pl.pallas_call(apply_kernel, in_specs=[vmem] * 9, out_specs=vmem, out_sha...  1.53 us
    unnamed x12, local copies, waits for them, and re-layouts  1.43 us
    pallas_call x1, Pallas kernels, slots_to_cells(): pl.pallas_call(slots_kernel, in_specs=[pl.BlockSpec(memory_space=pltpu.SM...  1.15 us
    pallas_call x1, Pallas kernels, edges(): pl.pallas_call(edges_kernel, grid=(2,), in_specs=[pl.BlockSpec((3, half *...  1.12 us
  transfers between devices with their start and end apart: 8, of which 3 were waited for; matrix products, arithmetic and copies ran while one was open for 0% of the time, Pallas kernels for 10%

commit v1 on v0

v1 whole, which is shorter than its diff:
```python
import functools

import jax
import jax.numpy as jnp
from jax import lax
from jax.experimental import pallas as pl
from jax.experimental.pallas import tpu as pltpu
from jax.sharding import PartitionSpec as P

STEPS = 4
F32 = jnp.float32
BF16 = jnp.bfloat16
HIGHEST = lax.Precision.HIGHEST
CH = 0.09
CU = 0.3
MIB = 1 << 20


def dot(a, b):
    return jnp.dot(a, b, preferred_element_type=F32, precision=HIGHEST)


def dot_t(a, b, precision=HIGHEST):
    return lax.dot_general(
        a, b, (((1,), (1,)), ((), ())), preferred_element_type=F32, precision=precision
    )


def edges_kernel(x_hbm, x_ref, first_ref, second_ref, sems):
    members, cols = first_ref.shape[2:]
    odd = lax.axis_index("grp")
    copies = [pltpu.make_async_copy(x_hbm.at[f], x_ref.at[f], sems.at[f]) for f in range(3)]
    for copy in copies:
        copy.start()
    for f in range(3):
        copies[f].wait()
        for out_ref, base in ((first_ref, STEPS * (1 - odd)), (second_ref, STEPS * odd)):
            for r in range(STEPS):
                for t in range(cols // 128):
                    q = x_ref[f, pl.ds(base + (t * 8 + r), members, stride=cols // 16), :]
                    out_ref[f, r, :, pl.ds(t * 128, 128)] = q.astype(BF16)


def edges(x, cols):
    members = x.shape[1] * 16 // cols
    shape = jax.ShapeDtypeStruct((3, STEPS, members, cols), BF16)
    return pl.pallas_call(
        edges_kernel,
        in_specs=[pl.BlockSpec(memory_space=pltpu.HBM)],
        out_specs=[pl.BlockSpec(memory_space=pltpu.VMEM)] * 3,
        out_shape=[jax.ShapeDtypeStruct(x.shape, F32), shape, shape],
        scratch_shapes=[pltpu.SemaphoreType.DMA((3,))],
        compiler_params=pltpu.CompilerParams(vmem_limit_bytes=16 * MIB),
        cost_estimate=pl.CostEstimate(flops=x.size, bytes_accessed=x.size * 6, transcendentals=0),
        name="edges",
    )(pltpu.with_memory_space_constraint(x, pltpu.HBM))


INNER = [(t, r) for t in range(STEPS) for r in range(t, 8 - t) if t or r in (0, 1, 6, 7)]


def advance_rows(load, store, rows):
    def north(q):
        return pltpu.roll(q, q.shape[1] - 1, axis=1)

    def south(q):
        return pltpu.roll(q, 1, axis=1)

    def terms(p):
        h, u, v = (load(f, p) for f in range(3))
        up, um = 0.25 + u, 0.25 - u
        flux = 0.5 * (u * u) + h
        quarter = 0.25 * u
        return dict(
            h=h, u=u, v=v, up=up, um=um,
            he=h * um, hw=h * up, ue=quarter - flux, uw=quarter + flux,
        )

    west, mid = terms(rows[0] - 1), terms(rows[0])
    for p in rows:
        east = terms(p + 1)
        h, u, v = mid["h"], mid["u"], mid["v"]
        vp, vm = 0.25 + v, 0.25 - v
        flux = 0.5 * (v * v) + h
        quarter = 0.25 * v
        store(0, p, (east["he"] + west["hw"]) + (north(h * vm) + south(h * vp)))
        store(1, p, (east["ue"] + west["uw"]) + (north(u) * vm + south(u) * vp) + 0.1 * v)
        store(
            2,
            p,
            (north(quarter - flux) + south(quarter + flux))
            + (east["v"] * mid["um"] + west["v"] * mid["up"])
            - 0.1 * u,
        )
        west, mid = mid, east


def inner_kernel(x_ref, inner_ref):
    members, cols = inner_ref.shape[2:]
    tiles, stride = cols // 128, cols // 16

    def group(g, _):
        part = pl.ds(pl.multiple_of(g * 8, 8), 8)
        base = pl.multiple_of(g * (8 * stride), 8 * stride)

        def load(f, p):
            q = jnp.concatenate(
                [x_ref[f, pl.ds(base + (t * 8 + p), 8, stride=stride), :] for t in range(tiles)],
                axis=1,
            )
            return q * CH + CH if f == 0 else q * CU

        for p in (0, 1, 6, 7):
            for f in range(3):
                inner_ref[f, INNER.index((0, p)), part, :] = load(f, p)
        for step in range(1, STEPS):

            def source(f, p):
                if step == 1:
                    return load(f, p)
                return inner_ref[f, INNER.index((step - 1, p)), part, :]

            def target(f, p, q):
                inner_ref[f, INNER.index((step, p)), part, :] = q

            advance_rows(source, target, range(step, 8 - step))
        return 0

    lax.fori_loop(0, members // 8, group, 0)


def inner_part(x, cols):
    members = x.shape[1] * 16 // cols
    vmem = pl.BlockSpec(memory_space=pltpu.VMEM)
    return pl.pallas_call(
        inner_kernel,
        in_specs=[vmem],
        out_specs=vmem,
        out_shape=jax.ShapeDtypeStruct((3, len(INNER), members, cols), F32),
        compiler_params=pltpu.CompilerParams(vmem_limit_bytes=32 * MIB),
        cost_estimate=pl.CostEstimate(flops=x.size * 50, bytes_accessed=x.size * 8, transcendentals=0),
        name="forecast_inner",
    )(x)


def side_kernel(second, plan, tiles, inner_ref, halo_ref, *refs):
    outs, (ping, pong, edge) = refs[-3 - len(plan) : -3], refs[-3:]
    before = refs[: -3 - len(plan)]
    members, cols = halo_ref.shape[2:]
    for f in range(3):
        for r in range(STEPS):
            q = halo_ref[f, r].astype(F32)
            edge[f, r] = q * CH + CH if f == 0 else q * CU

    def side(above):
        def first_row(t):
            return 8 - t if above else t - STEPS

        def group(g, _):
            part = pl.ds(pl.multiple_of(g * 8, 8), 8)
            for step in range(1, STEPS + 1):
                source_ref, target_ref = (ping, pong) if step % 2 else (pong, ping)

                def source(f, p):
                    if step - 1 <= p < 9 - step:
                        return inner_ref[f, INNER.index((step - 1, p)), part, :]
                    if step == 1:
                        return edge[f, p - 8 if above else p + STEPS, part, :]
                    return source_ref[f, p - first_row(step - 1), part, :]

                def target(f, p, q):
                    target_ref[f, p - first_row(step), part, :] = q

                advance_rows(source, target, range(first_row(step), first_row(step) + STEPS))
            return 0

        lax.fori_loop(0, members // 8, group, 0)

    from_above = lax.axis_index("grp") == (1 if second else 0)
    pl.when(from_above)(lambda: side(True))
    pl.when(jnp.logical_not(from_above))(lambda: side(False))
    last = ping if STEPS % 2 == 0 else pong
    rank = lax.axis_index("mem")
    for (shift, fields), out_ref in zip(plan, outs):
        base = out_ref.shape[1] - STEPS
        part = pl.ds(pl.multiple_of(lax.rem(rank + shift, tiles) * 128, 128), 128)
        for k, f in enumerate(fields):
            if base:
                out_ref[k, :STEPS] = before[shift][f]
            for r in range(STEPS):
                q = last[f, r, :, part]
                q = q * (1.0 / CH) - 1.0 if f == 0 else q * (1.0 / CU)
                out_ref[k, base + r] = q.astype(BF16)


def side_part(inner, halo, second, plan, tiles, before=()):
    members, cols = halo.shape[2:]
    vmem = pl.BlockSpec(memory_space=pltpu.VMEM)
    rows = [STEPS if shift == 0 or not second else 2 * STEPS for shift, _ in plan]
    return pl.pallas_call(
        functools.partial(side_kernel, second, plan, tiles),
        in_specs=[vmem] * (2 + len(before)),
        out_specs=[vmem] * len(plan),
        out_shape=[
            jax.ShapeDtypeStruct((len(fields), n, members, 128), BF16)
            for n, (_, fields) in zip(rows, plan)
        ],
        scratch_shapes=[pltpu.VMEM((3, STEPS, members, cols), F32)] * 3,
        compiler_params=pltpu.CompilerParams(vmem_limit_bytes=24 * MIB),
        cost_estimate=pl.CostEstimate(
            flops=halo.size * 160, bytes_accessed=halo.size * 16, transcendentals=0
        ),
        name="forecast_second" if second else "forecast_first",
    )(inner, halo, *before)


def slots_kernel(count_ref, cells_ref, values_ref, error_ref, noise_ref, z_ref, omega_ref, lhs):
    slots = cells_ref.shape[1]
    members = noise_ref.shape[1]
    error = error_ref[...]
    live = lax.broadcasted_iota(jnp.int32, (1, slots), 1) < count_ref[0, 0]
    weight = jnp.where(live, 1.0 / (error * error), 0.0)
    rows = members + 16

    def put(at, size, cols, value):
        high = value.astype(BF16)
        rest = value - high.astype(F32)
        middle = rest.astype(BF16)
        low = (rest - middle.astype(F32)).astype(BF16)
        for k, q in enumerate((high, middle, low)):
            lhs[pl.ds(k * rows + at, size), cols] = q

    for b in range(slots // 128):
        part = pl.ds(b * 128, 128)
        lane = slice(b * 128, (b + 1) * 128)
        innovation = values_ref[:, part] + error[:, lane] * noise_ref[part, :].T
        put(0, members, part, weight[:, lane] * innovation)
    put(members, 16, pl.ds(0, slots), jnp.broadcast_to(weight, (16, slots)))
    block = 256
    cells = cells_ref[...]
    for b in range(z_ref.shape[1] // block):
        ids = lax.broadcasted_iota(jnp.int32, (block, slots), 0) + b * block
        chosen = jnp.where(ids == cells, 1.0, 0.0).astype(BF16)
        total = lax.dot_general(
            lhs[...], chosen, (((1,), (1,)), ((), ())), preferred_element_type=F32
        )
        total = total[:rows] + (total[rows : 2 * rows] + total[2 * rows :])
        part = pl.ds(b * block, block)
        z_ref[:, part] = total[:members]
        omega_ref[:, part] = total[members : members + 8]


def slots_to_cells(count, cells, values, error, noise):
    slots, members = noise.shape
    vmem = pl.BlockSpec(memory_space=pltpu.VMEM)
    return pl.pallas_call(
        slots_kernel,
        in_specs=[pl.BlockSpec(memory_space=pltpu.SMEM)] + [vmem] * 4,
        out_specs=[vmem, vmem],
        out_shape=[
            jax.ShapeDtypeStruct((members, 1024), F32),
            jax.ShapeDtypeStruct((8, 1024), F32),
        ],
        scratch_shapes=[pltpu.VMEM((3 * (members + 16), slots), BF16)],
        compiler_params=pltpu.CompilerParams(vmem_limit_bytes=32 * MIB),
        cost_estimate=pl.CostEstimate(
            flops=4 * members * slots * 1024, bytes_accessed=8 * noise.size, transcendentals=0
        ),
        name="slots_to_cells",
    )(count, cells, values, error, noise)


def split(a):
    high = a.astype(BF16)
    return high, (a - high.astype(F32)).astype(BF16)


def half_bases():
    odd = lax.axis_index("grp")
    return STEPS * (1 - odd), STEPS * odd


def piece(refs, where, s, f, half, r):
    array, field, row = where[s][f][half]
    return refs[array][field, row + r]


def weights_kernel(where, z_ref, omega_ref, *refs):
    parts, (w_ref, x_ref, t_ref, q_ref) = refs[:-4], refs[-4:]
    devices = len(where)
    size = parts[0].shape[2]
    members = size * devices
    for half, base in enumerate(half_bases()):
        for r in range(STEPS):
            lanes = pl.ds(pl.multiple_of((base + r) * 128, 128), 128)
            for s in range(devices):
                x_ref[pl.ds(s * size, size), lanes] = piece(parts, where, s, 0, half, r).astype(F32)
    x = x_ref[...]
    mean = jnp.sum(x, axis=0, keepdims=True) * (1.0 / members)
    x = x - mean
    omega = omega_ref[pl.ds(0, 1), :]
    left_high, left_low = split(jnp.concatenate([x * omega, z_ref[...] - omega * mean], axis=0))
    high, low = split(x)
    both = dot_t(left_high, high, None) + (
        dot_t(left_high, low, None) + dot_t(left_low, high, None)
    )
    shape = (members, members)
    down = lax.broadcasted_iota(jnp.int32, shape, 0)
    across = lax.broadcasted_iota(jnp.int32, shape, 1)
    eye = jnp.where(down == across, 1.0, 0.0)
    rank = lax.axis_index("mem")
    member = lax.rem(rank + devices - across // size, devices) * size + lax.rem(across, size)
    own = jnp.where(down == member, 1.0, 0.0)
    diagonal = members - 1.0
    gram = both[:members]
    rhs = both[members:] + diagonal * own
    square = dot(gram, gram)
    gram = gram + diagonal * eye
    top = jnp.sqrt(jnp.sqrt(jnp.sum(square * square)))
    low = 0.98 * diagonal
    high = 1.01 * (diagonal + top)
    inv = 1.0 / (high - low)
    z = (high + low) * inv
    alpha = (high + low - 2.0 * diagonal) * inv
    beta = 2.0 * inv
    less = gram - diagonal * eye
    t1 = alpha * eye - beta * less
    t2 = (2.0 * alpha * alpha - 1.0) * eye - (4.0 * alpha * beta) * less + (2.0 * beta * beta) * square
    z2 = 2.0 * z * z - 1.0
    t_ref[...] = t2
    q_ref[...] = (2.0 / (high + low)) * (2.0 * z / z2) * (z * eye + t1)

    def double(t):
        cheb, q = t_ref[...], q_ref[...]
        after = 2.0 * t * t - 1.0
        q_ref[...] = (2.0 * t / after) * (t * q + dot(q, cheb))
        t_ref[...] = 2.0 * dot(cheb, cheb) - eye
        return after

    lax.while_loop(lambda t: t < 3000.0, double, z2)
    inverse = q_ref[...]
    w = dot(rhs, inverse)
    w = w + dot(rhs - dot(w, gram), inverse)
    w_ref[:, pl.ds(0, members)], w_ref[:, pl.ds(members, members)] = split(w)


def weights(z, omega, where, arrays):
    members = z.shape[0]
    vmem = pl.BlockSpec(memory_space=pltpu.VMEM)
    return pl.pallas_call(
        functools.partial(weights_kernel, where),
        in_specs=[vmem] * (2 + len(arrays)),
        out_specs=vmem,
        out_shape=jax.ShapeDtypeStruct((members, 2 * members), BF16),
        scratch_shapes=[
            pltpu.VMEM((members, 1024), F32),
            pltpu.VMEM((members, members), F32),
            pltpu.VMEM((members, members), F32),
        ],
        compiler_params=pltpu.CompilerParams(vmem_limit_bytes=24 * MIB),
        cost_estimate=pl.CostEstimate(
            flops=4000 * members**3, bytes_accessed=8 * z.size, transcendentals=0
        ),
        name="weights",
    )(z, omega, *arrays)


def apply_kernel(where, w_ref, *refs):
    parts, (out_hbm, stage, out_ref, sems) = refs[:-4], refs[-4:]
    devices = len(where)
    members = w_ref.shape[0]
    w = w_ref[...]
    copies = []
    for f in range(3):
        for half, base in enumerate(half_bases()):
            for r in range(0, STEPS, 2):
                pair = []
                for k in (r, r + 1):
                    pieces = [piece(parts, where, s, f, half, k) for s in range(devices)]
                    pair.append(jnp.concatenate(pieces + pieces, axis=0))
                both = jnp.dot(w, jnp.concatenate(pair, axis=1), preferred_element_type=F32)
                for k in range(2):
                    rows = pl.ds(base + (r + k), members, stride=8)
                    stage[f % 2, rows, :] = both[:, k * 128 : (k + 1) * 128]
        out_ref[f] = stage[f % 2].astype(BF16)
        copies.append(pltpu.make_async_copy(out_ref.at[f], out_hbm.at[f], sems.at[f]))
        copies[-1].start()
    for copy in copies:
        copy.wait()


def apply_weights(w, where, arrays):
    members = w.shape[0]
    vmem = pl.BlockSpec(memory_space=pltpu.VMEM)
    shape = (3, members * 8, 128)
    return pl.pallas_call(
        functools.partial(apply_kernel, where),
        in_specs=[vmem] * (1 + len(arrays)),
        out_specs=pl.BlockSpec(memory_space=pltpu.HBM),
        out_shape=jax.ShapeDtypeStruct(shape, BF16),
        scratch_shapes=[
            pltpu.VMEM((2, members * 8, 128), F32),
            pltpu.VMEM(shape, BF16),
            pltpu.SemaphoreType.DMA((3,)),
        ],
        compiler_params=pltpu.CompilerParams(vmem_limit_bytes=24 * MIB),
        cost_estimate=pl.CostEstimate(
            flops=12 * members * members * 1024, bytes_accessed=12 * members * 1024, transcendentals=0
        ),
        name="apply_weights",
    )(w, *arrays)


def send(x, shift):
    size = lax.axis_size("mem")
    return lax.ppermute(x, "mem", [(i, (i + shift) % size) for i in range(size)])


def body(members, obs_cells, obs_count, obs_values, obs_error, obs_noise):
    fields, count, lines, cols = members.shape
    x = members.reshape(fields, count, lines, cols // 128, 128)
    x = x.transpose(0, 1, 3, 2, 4).reshape(fields, -1, 128)
    x, first, second = edges(x, cols)
    slabs = lax.axis_size("tile") * lax.axis_size("grp")
    beyond = [(s, (s + 1 if s % 2 else s - 1) % slabs) for s in range(slabs)]
    halo_first = lax.ppermute(first, "grp", [(0, 1), (1, 0)])
    halo_second = lax.ppermute(second, ("tile", "grp"), beyond)
    inner = inner_part(x, cols)
    slots = obs_cells.shape[-1]
    obs_count, inner = lax.optimization_barrier((obs_count, inner))
    z, omega = slots_to_cells(
        obs_count,
        obs_cells.reshape(1, slots),
        obs_values.reshape(1, slots),
        obs_error.reshape(1, slots),
        obs_noise.reshape(slots, -1),
    )
    halo_first, z, omega = lax.optimization_barrier((halo_first, z, omega))
    size = lax.axis_size("mem")
    every = tuple(range(fields))
    early = side_part(inner, halo_first, False, tuple((s, every) for s in range(size)), size)
    far = size // 2
    near = [s for s in range(1, size) if s != far]
    plan = [(0, every), (far, every)] + [(s, (0,)) for s in near] + [(s, every[1:]) for s in near]
    late = side_part(inner, halo_second, True, tuple(plan), size, early)
    arrays = [early[0]]
    where = [[None] * fields for _ in range(size)]
    for k, ((shift, held), block) in enumerate(zip(plan, late)):
        arrays.append(send(block, shift) if shift else block)
        for i, f in enumerate(held):
            where[shift][f] = ((k + 1, i, 0), (k + 1, i, STEPS)) if shift else ((0, f, 0), (1, f, 0))
    needed = 3 + len(near)
    w = weights(z, omega, where, arrays[:needed])
    out = apply_weights(w, where, arrays)
    return out.reshape(fields, -1, lines, 128)


def solution(mesh):
    in_specs = (
        P(None, "mem", ("tile", "grp"), None),
        P(("tile", "grp"), "mem", None),
        P(("tile", "grp"), "mem"),
        P(("tile", "grp"), "mem", None),
        P(("tile", "grp"), "mem", None),
        P(("tile", "grp"), "mem", None, None),
    )
    out_specs = P(None, None, ("tile", "grp"), "mem")
    return jax.shard_map(body, mesh=mesh, in_specs=in_specs, out_specs=out_specs, check_vma=False)
```

time: 42.9 us -> 34.7 us (0.81)
  waiting for transfers between devices: 11.3 us -> 3.94 us
  Pallas kernels: 12.9 us -> 14.5 us
  local copies, waits for them, and re-layouts: 1.49 us -> 0.03 us
  starting transfers between devices: 16 us -> 15.3 us
    ppermute x8 -> x7, waiting for transfers between devices: 11.3 us -> 3.94 us  [the longest x5 3.93 us: send(): lax.ppermute(x, 'mem', [(i, (i + shift) % size) for i in range(size)])]
    pallas_call x4 -> x6, Pallas kernels: 11.7 us -> 13.3 us  [the longest x2 4.58 us: side_part(): pl.pallas_call(functools.partial(side_kernel, second, plan, tiles), in_sp...]
    unnamed x12 -> x8, local copies, waits for them, and re-layouts: 1.43 us -> 0.03 us
    ppermute x8 -> x7, starting transfers between devices: 16 us -> 15.3 us  [the longest x5 6.97 us: send(): lax.ppermute(x, 'mem', [(i, (i + shift) % size) for i in range(size)])]
  transfers between devices with their start and end apart: 8 -> 7, of which waited for: 3 -> 1; matrix products, arithmetic and copies ran while one was open for 0% -> 0% of each run, Pallas kernels for 10% -> 25%
where the time goes in v1:
time: 34.7 us; the launch traced here: 34.5 us
  starting transfers between devices  15.3 us (44%)
  Pallas kernels  14.5 us (42%)
  waiting for transfers between devices  3.94 us (11%)
  between operations  0.8 us (2%)
    ppermute x5, starting transfers between devices, send(): lax.ppermute(x, 'mem', [(i, (i + shift) % size) for i in range(size)])  6.97 us
    ppermute x1, starting transfers between devices, body(): halo_second = lax.ppermute(second, ('tile', 'grp'), beyond)  6.3 us
    pallas_call x2, Pallas kernels, side_part(): pl.pallas_call(functools.partial(side_kernel, second, plan, tiles), in_sp...  4.58 us
    ppermute x5, waiting for transfers between devices, send(): lax.ppermute(x, 'mem', [(i, (i + shift) % size) for i in range(size)])  3.93 us
    pallas_call x1, Pallas kernels, weights(): pl.pallas_call(functools.partial(weights_kernel, where), in_specs=[vmem]...  2.94 us
    pallas_call x1, Pallas kernels, inner_part(): pl.pallas_call(inner_kernel, in_specs=[vmem], out_specs=vmem, out_shape=j...  2.47 us
    ppermute x1, starting transfers between devices, body(): halo_first = lax.ppermute(first, 'grp', [(0, 1), (1, 0)])  2 us
    pallas_call x1, Pallas kernels, edges(): pl.pallas_call(edges_kernel, in_specs=[pl.BlockSpec(memory_space=pltpu.HB...  1.99 us
  transfers between devices with their start and end apart: 7, of which 1 were waited for; matrix products, arithmetic and copies ran while one was open for 0% of the time, Pallas kernels for 25%

profile of v1, /device:TPU:8, one launch (start us, length us, event | category | flops | bytes accessed | tf_op | source)
XLA Modules:
  0.0 34.5 jit_solution(14224990797453434852)
XLA Ops:
  0.0 2.0 %edges.1 = (f32[3,1024,128]{2,1,0:T(8,128)S(1)}, bf16[3,4,32,512]{3,2,1,0:T(8,128)(2,1)S(1)}, bf16[3,4,32,512]{3,2,1,0:T(8,128)(2,1)S(1)}) custom-call(f32[3,1024,128]{2,1,0:T(8,128)} %bitcast.14), custom_call_target="tpu_custom_call" | custom-call | flops 393216 | bytes 2359296 | tf_op jit(solution)/shard_map/edges/pallas_call | solution.py:47
  2.0 2.0 %collective-permute-start = (bf16[3,4,32,512]{3,2,1,0:T(8,128)(2,1)S(1)}, bf16[3,4,32,512]{3,2,1,0:T(8,128)(2,1)S(1)}, u32[]{:S(2)}, u32[]{:S(2)}) collective-permute-start(bf16[3,4,32,512]{3,2,1,0:T(8,128)(2,1)S(1)} %get-tuple-element.25), channel_id=1, source_target_pairs={{0,1},{1,0},{2,3},{3,2},{4,5},{5,4},{6,7},{7,6},{8,9},{9,8},{10,11... | collective-permute-start | bytes 1179656 | tf_op jit(solution)/shard_map/ppermute | solution.py:426
  4.0 6.3 %collective-permute-start.1 = (bf16[3,4,32,512]{3,2,1,0:T(8,128)(2,1)S(1)}, bf16[3,4,32,512]{3,2,1,0:T(8,128)(2,1)S(1)}, u32[]{:S(2)}, u32[]{:S(2)}) collective-permute-start(bf16[3,4,32,512]{3,2,1,0:T(8,128)(2,1)S(1)} %get-tuple-element.35), channel_id=1, source_target_pairs={{0,63},{1,2},{2,1},{3,4},{4,3},{5,6},{6,5},{7,8},{8,7},{9,10},{10,... | collective-permute-start | bytes 1179656 | tf_op jit(solution)/shard_map/ppermute | solution.py:427
  11.0 0.0 copy-start
  11.0 0.0 copy-start.1
  11.0 0.0 copy-start.2
  11.0 0.0 copy-start.3
  11.0 2.5 %forecast_inner.1.inner_ref = f32[3,16,32,512]{3,2,1,0:T(8,128)S(1)} custom-call(f32[3,1024,128]{2,1,0:T(8,128)S(1)} %get-tuple-element.26.x_ref), custom_call_target="tpu_custom_call" | custom-call | flops 19660800 | bytes 3145728 | tf_op jit(solution)/shard_map/forecast_inner/pallas_call | solution.py:135
  13.5 0.0 copy-done
  13.5 0.0 copy-done.1
  13.5 0.0 copy-done.2
  13.5 0.0 copy-done.3
  13.5 1.2 %slots_to_cells.1 = (f32[128,1024]{1,0:T(8,128)S(1)}, f32[8,1024]{1,0:T(8,128)S(1)}) custom-call(s32[1,1]{1,0:T(1,128)S(6)} %copy.7.count_ref, s32[1,1024]{1,0:T(1,128)S(1)} %bitcast.11, f32[1,1024]{1,0:T(1,128)S(1)} %bitcast.12, f32[1,1024]{1,0:T(1,128)S(1)} %bitcast.13, f32[1024,128]{1,0:T(8,128)S(1)} %bitcast.10), custom_call_target="tpu_custom_call" | custom-call | flops 536870912 | bytes 1048576 | tf_op jit(solution)/shard_map/slots_to_cells/pallas_call | solution.py:256
  14.7 0.0 collective-permute-done.halo_ref
  14.7 2.2 %forecast_first.1 = (bf16[3,4,32,128]{3,2,1,0:T(8,128)(2,1)S(1)}, bf16[3,4,32,128]{3,2,1,0:T(8,128)(2,1)S(1)}, bf16[3,4,32,128]{3,2,1,0:T(8,128)(2,1)S(1)}, bf16[3,4,32,128]{3,2,1,0:T(8,128)(2,1)S(1)}) custom-call(f32[3,16,32,512]{3,2,1,0:T(8,128)S(1)} %forecast_inner.1.inner_ref, bf16[3,4,32,512]{3,2,1,0:T(8,128)(2,1)S(1)} %collective-permute-done.halo_ref), custom_call_target="tpu_custom_call" | custom-call | flops 31457280 | bytes 3145728 | tf_op jit(solution)/shard_map/forecast_first/pallas_call | solution.py:200
  16.9 0.0 collective-permute-done.1.halo_ref
  16.9 2.4 %forecast_second.1 = (bf16[3,4,32,128]{3,2,1,0:T(8,128)(2,1)S(1)}, bf16[3,8,32,128]{3,2,1,0:T(8,128)(2,1)S(1)}, bf16[1,8,32,128]{3,2,1,0:T(8,128)(2,1)S(1)}, bf1...) custom-call(f32[3,16,32,512]{3,2,1,0:T(8,128)S(1)} %forecast_inner.1.inner, ...), custom_call_target="tpu_custom_call" | custom-call | flops 31457280 | bytes 3145728 | tf_op jit(solution)/shard_map/forecast_second/pallas_call | solution.py:200
  19.3 2.4 %collective-permute-start.2 = (bf16[3,8,32,128]{3,2,1,0:T(8,128)(2,1)S(1)}, bf16[3,8,32,128]{3,2,1,0:T(8,128)(2,1)S(1)}, u32[]{:S(2)}, u32[]{:S(2)}) collective-permute-start(bf16[3,8,32,128]{3,2,1,0:T(8,128)(2,1)S(1)} %get-tuple-element.40), channel_id=1, source_target_pairs={{0,128},{64,192},{128,0},{192,64},{1,129},{65,193},{129,1},{193,65... | collective-permute-start | bytes 589832 | tf_op jit(solution)/shard_map/ppermute | solution.py:416
  21.7 0.0 collective-permute-start.3
  21.7 2.0 %collective-permute-start.4 = (bf16[1,8,32,128]{3,2,1,0:T(8,128)(2,1)S(1)}, bf16[1,8,32,128]{3,2,1,0:T(8,128)(2,1)S(1)}, u32[]{:S(2)}, u32[]{:S(2)}) collective-permute-start(bf16[1,8,32,128]{3,2,1,0:T(8,128)(2,1)S(1)} %get-tuple-element.42), channel_id=1, source_target_pairs={{0,192},{64,0},{128,64},{192,128},{1,193},{65,1},{129,65},{193,129... | collective-permute-start | bytes 196616 | tf_op jit(solution)/shard_map/ppermute | solution.py:416
  23.7 0.0 collective-permute-start.5
  23.7 2.6 %collective-permute-start.6 = (bf16[2,8,32,128]{3,2,1,0:T(8,128)(2,1)S(1)}, bf16[2,8,32,128]{3,2,1,0:T(8,128)(2,1)S(1)}, u32[]{:S(2)}, u32[]{:S(2)}) collective-permute-start(bf16[2,8,32,128]{3,2,1,0:T(8,128)(2,1)S(1)} %get-tuple-element.44), channel_id=1, source_target_pairs={{0,192},{64,0},{128,64},{192,128},{1,193},{65,1},{129,65},{193,129... | collective-permute-start | bytes 393224 | tf_op jit(solution)/shard_map/ppermute | solution.py:416
  26.3 3.9 %collective-permute-done.3.refs_3_ = bf16[1,8,32,128]{3,2,1,0:T(8,128)(2,1)S(1)} collective-permute-done((bf16[1,8,32,128]{3,2,1,0:T(8,128)(2,1)S(1)}, bf16[1,8,32,128]{3,2,1,0:T(8,128)(2,1)S(1)}, u32[]{:S(2)}, u32[]{:S(2)}) %collective-permute-start.3) | collective-permute-done | bytes 65568 | tf_op jit(solution)/shard_map/ppermute | solution.py:416
  30.2 0.0 collective-permute-done.4.refs_4_
  30.2 0.0 collective-permute-done.2.refs_2_
  30.2 2.9 %weights.1.w_ref = bf16[128,256]{1,0:T(8,128)(2,1)S(1)} custom-call(f32[128,1024]{1,0:T(8,128)S(1)} %get-tuple-element.30.z_ref, f32[8,1024]{1,0:T(8,128)S(1)} %get-tuple-element.31.omega_ref, bf16[3,4,32,128]{3,2,1,0:T(8,128)(2,1)S(1)} %get-tuple-element.34.refs_0_, bf16[3,4,32,128]{3,2,1,0:T(8,128)(2,1)S(1)} %get-tuple-element.39.refs_1_, ...), custom_call_target="tpu_custom_call" | custom-call | flops 8388608000 | bytes 1048576 | tf_op jit(solution)/shard_map/weights/pallas_call | solution.py:350
  33.1 0.0 collective-permute-done.5.refs_5_
  33.2 0.0 collective-permute-done.6.refs_6_
  33.2 1.4 %apply_weights.1 = bf16[3,1024,128]{2,1,0:T(8,128)(2,1)} custom-call(bf16[128,256]{1,0:T(8,128)(2,1)S(1)} %weights.1.w_ref, bf16[3,4,32,128]{3,2,1,0:T(8,128)(2,1)S(1)} %get-tuple-element.34.refs_0_, bf16[3,4,32,128]{3,2,1,0:T(8,128)(2,1)S(1)} %get-tuple-element.39.refs_1_, bf16[3,8,32,128]{3,2,1,0:T(8,128)(2,1)S(1)} %collective-permute-done.2.refs_2_, ...), custom_call_target="tpu_custom_call" | custom-call | flops 201326592 | bytes 1572864 | tf_op jit(solution)/shard_map/apply_weights/pallas_call | solution.py:396
Async XLA Ops:
  2.0 12.7 %collective-permute-start = (bf16[3,4,32,512]{3,2,1,0:T(8,128)(2,1)S(1)}, bf16[3,4,32,512]{3,2,1,0:T(8,128)(2,1)S(1)}, u32[]{:S(2)}, u32[]{:S(2)}) collective-permute-start(bf16[3,4,32,512]{3,2,1,0:T(8,128)(2,1)S(1)} %get-tuple-element.25), channel_id=1, source_target_pairs={{0,1},{1,0},{2,3},{3,2},{4,5},{5,4},{6,7},{7,6},{8,9},{9,8},{10,11... | collective-permute-start | bytes 1179656 | tf_op jit(solution)/shard_map/ppermute | solution.py:426
  4.0 12.9 %collective-permute-start.1 = (bf16[3,4,32,512]{3,2,1,0:T(8,128)(2,1)S(1)}, bf16[3,4,32,512]{3,2,1,0:T(8,128)(2,1)S(1)}, u32[]{:S(2)}, u32[]{:S(2)}) collective-permute-start(bf16[3,4,32,512]{3,2,1,0:T(8,128)(2,1)S(1)} %get-tuple-element.35), channel_id=1, source_target_pairs={{0,63},{1,2},{2,1},{3,4},{4,3},{5,6},{6,5},{7,8},{8,7},{9,10},{10,... | collective-permute-start | bytes 1179656 | tf_op jit(solution)/shard_map/ppermute | solution.py:427
  11.0 2.5 %copy-start = (f32[1,1,1024,128]{3,2,1,0:T(8,128)S(1)}, f32[1,1,1024,128]{3,2,1,0:T(8,128)}, u32[]{:S(2)}) copy-start(f32[1,1,1024,128]{3,2,1,0:T(8,128)} %param.11) | copy-start | bytes 1572868
  11.0 2.5 %copy-start.1 = (s32[1,1,1024]{2,1,0:T(1,128)S(1)}, s32[1,1,1024]{2,1,0:T(1,128)}, u32[]{:S(2)}) copy-start(s32[1,1,1024]{2,1,0:T(1,128)} %param.7) | copy-start | bytes 12292
  11.0 2.5 %copy-start.2 = (f32[1,1,1024]{2,1,0:T(1,128)S(1)}, f32[1,1,1024]{2,1,0:T(1,128)}, u32[]{:S(2)}) copy-start(f32[1,1,1024]{2,1,0:T(1,128)} %param.9) | copy-start | bytes 12292
  11.0 2.5 %copy-start.3 = (f32[1,1,1024]{2,1,0:T(1,128)S(1)}, f32[1,1,1024]{2,1,0:T(1,128)}, u32[]{:S(2)}) copy-start(f32[1,1,1024]{2,1,0:T(1,128)} %param.10) | copy-start | bytes 12292
  19.3 10.9 %collective-permute-start.2 = (bf16[3,8,32,128]{3,2,1,0:T(8,128)(2,1)S(1)}, bf16[3,8,32,128]{3,2,1,0:T(8,128)(2,1)S(1)}, u32[]{:S(2)}, u32[]{:S(2)}) collective-permute-start(bf16[3,8,32,128]{3,2,1,0:T(8,128)(2,1)S(1)} %get-tuple-element.40), channel_id=1, source_target_pairs={{0,128},{64,192},{128,0},{192,64},{1,129},{65,193},{129,1},{193,65... | collective-permute-start | bytes 589832 | tf_op jit(solution)/shard_map/ppermute | solution.py:416
  21.7 8.5 %collective-permute-start.3 = (bf16[1,8,32,128]{3,2,1,0:T(8,128)(2,1)S(1)}, bf16[1,8,32,128]{3,2,1,0:T(8,128)(2,1)S(1)}, u32[]{:S(2)}, u32[]{:S(2)}) collective-permute-start(bf16[1,8,32,128]{3,2,1,0:T(8,128)(2,1)S(1)} %get-tuple-element.41), channel_id=1, source_target_pairs={{0,64},{64,128},{128,192},{192,0},{1,65},{65,129},{129,193},{193,1... | collective-permute-start | bytes 196616 | tf_op jit(solution)/shard_map/ppermute | solution.py:416
  21.7 8.5 %collective-permute-start.4 = (bf16[1,8,32,128]{3,2,1,0:T(8,128)(2,1)S(1)}, bf16[1,8,32,128]{3,2,1,0:T(8,128)(2,1)S(1)}, u32[]{:S(2)}, u32[]{:S(2)}) collective-permute-start(bf16[1,8,32,128]{3,2,1,0:T(8,128)(2,1)S(1)} %get-tuple-element.42), channel_id=1, source_target_pairs={{0,192},{64,0},{128,64},{192,128},{1,193},{65,1},{129,65},{193,129... | collective-permute-start | bytes 196616 | tf_op jit(solution)/shard_map/ppermute | solution.py:416
  23.7 9.4 %collective-permute-start.5 = (bf16[2,8,32,128]{3,2,1,0:T(8,128)(2,1)S(1)}, bf16[2,8,32,128]{3,2,1,0:T(8,128)(2,1)S(1)}, u32[]{:S(2)}, u32[]{:S(2)}) collective-permute-start(bf16[2,8,32,128]{3,2,1,0:T(8,128)(2,1)S(1)} %get-tuple-element.43), channel_id=1, source_target_pairs={{0,64},{64,128},{128,192},{192,0},{1,65},{65,129},{129,193},{193,1... | collective-permute-start | bytes 393224 | tf_op jit(solution)/shard_map/ppermute | solution.py:416
  23.7 9.4 %collective-permute-start.6 = (bf16[2,8,32,128]{3,2,1,0:T(8,128)(2,1)S(1)}, bf16[2,8,32,128]{3,2,1,0:T(8,128)(2,1)S(1)}, u32[]{:S(2)}, u32[]{:S(2)}) collective-permute-start(bf16[2,8,32,128]{3,2,1,0:T(8,128)(2,1)S(1)} %get-tuple-element.44), channel_id=1, source_target_pairs={{0,192},{64,0},{128,64},{192,128},{1,193},{65,1},{129,65},{193,129... | collective-permute-start | bytes 393224 | tf_op jit(solution)/shard_map/ppermute | solution.py:416

commit v2 on v1

--- a/solution.py
+++ b/solution.py
@@ -183,7 +183,7 @@
     rank = lax.axis_index("mem")
     for (shift, fields), out_ref in zip(plan, outs):
         base = out_ref.shape[1] - STEPS
-        part = pl.ds(pl.multiple_of(lax.rem(rank + shift, tiles) * 128, 128), 128)
+        part = pl.ds(pl.multiple_of(lax.bitwise_xor(rank, shift) * 128, 128), 128)
         for k, f in enumerate(fields):
             if base:
                 out_ref[k, :STEPS] = before[shift][f]
@@ -309,7 +309,7 @@
     across = lax.broadcasted_iota(jnp.int32, shape, 1)
     eye = jnp.where(down == across, 1.0, 0.0)
     rank = lax.axis_index("mem")
-    member = lax.rem(rank + devices - across // size, devices) * size + lax.rem(across, size)
+    member = lax.bitwise_xor(across // size, rank) * size + lax.rem(across, size)
     own = jnp.where(down == member, 1.0, 0.0)
     diagonal = members - 1.0
     gram = both[:members]
@@ -413,7 +413,7 @@
 
 def send(x, shift):
     size = lax.axis_size("mem")
-    return lax.ppermute(x, "mem", [(i, (i + shift) % size) for i in range(size)])
+    return lax.ppermute(x, "mem", [(i, i ^ shift) for i in range(size)])
 
 
 def body(members, obs_cells, obs_count, obs_values, obs_error, obs_noise):

time: 34.7 us -> 34.5 us (level)
  no operation moved by 1% of the time
where the time goes in v2:
time: 34.5 us; the launch traced here: 34.2 us
  starting transfers between devices  15.3 us (44%)
  Pallas kernels  14.2 us (41%)
  waiting for transfers between devices  3.86 us (11%)
  between operations  0.8 us (2%)
    ppermute x5, starting transfers between devices, send(): return lax.ppermute(x, 'mem', [(i, i ^ shift) for i in range(size)])  7.04 us
    ppermute x1, starting transfers between devices, body(): halo_second = lax.ppermute(second, ('tile', 'grp'), beyond)  6.3 us
    pallas_call x2, Pallas kernels, side_part(): pl.pallas_call(functools.partial(side_kernel, second, plan, tiles), in_sp...  4.58 us
    ppermute x5, waiting for transfers between devices, send(): return lax.ppermute(x, 'mem', [(i, i ^ shift) for i in range(size)])  3.86 us
    pallas_call x1, Pallas kernels, weights(): pl.pallas_call(functools.partial(weights_kernel, where), in_specs=[vmem]...  2.67 us
    pallas_call x1, Pallas kernels, inner_part(): pl.pallas_call(inner_kernel, in_specs=[vmem], out_specs=vmem, out_shape=j...  2.47 us
    ppermute x1, starting transfers between devices, body(): halo_first = lax.ppermute(first, 'grp', [(0, 1), (1, 0)])  2 us
    pallas_call x1, Pallas kernels, edges(): pl.pallas_call(edges_kernel, in_specs=[pl.BlockSpec(memory_space=pltpu.HB...  1.99 us
  transfers between devices with their start and end apart: 7, of which 1 were waited for; matrix products, arithmetic and copies ran while one was open for 0% of the time, Pallas kernels for 25%

profile of v2, /device:TPU:8, one launch (start us, length us, event | category | flops | bytes accessed | tf_op | source)
XLA Modules:
  0.0 34.2 jit_solution(2244599788310964885)
XLA Ops:
  0.0 2.0 %edges.1 = (f32[3,1024,128]{2,1,0:T(8,128)S(1)}, bf16[3,4,32,512]{3,2,1,0:T(8,128)(2,1)S(1)}, bf16[3,4,32,512]{3,2,1,0:T(8,128)(2,1)S(1)}) custom-call(f32[3,1024,128]{2,1,0:T(8,128)} %bitcast.14), custom_call_target="tpu_custom_call" | custom-call | flops 393216 | bytes 2359296 | tf_op jit(solution)/shard_map/edges/pallas_call | solution.py:47
  2.0 2.0 %collective-permute-start = (bf16[3,4,32,512]{3,2,1,0:T(8,128)(2,1)S(1)}, bf16[3,4,32,512]{3,2,1,0:T(8,128)(2,1)S(1)}, u32[]{:S(2)}, u32[]{:S(2)}) collective-permute-start(bf16[3,4,32,512]{3,2,1,0:T(8,128)(2,1)S(1)} %get-tuple-element.25), channel_id=1, source_target_pairs={{0,1},{1,0},{2,3},{3,2},{4,5},{5,4},{6,7},{7,6},{8,9},{9,8},{10,11... | collective-permute-start | bytes 1179656 | tf_op jit(solution)/shard_map/ppermute | solution.py:426
  4.0 6.3 %collective-permute-start.1 = (bf16[3,4,32,512]{3,2,1,0:T(8,128)(2,1)S(1)}, bf16[3,4,32,512]{3,2,1,0:T(8,128)(2,1)S(1)}, u32[]{:S(2)}, u32[]{:S(2)}) collective-permute-start(bf16[3,4,32,512]{3,2,1,0:T(8,128)(2,1)S(1)} %get-tuple-element.35), channel_id=1, source_target_pairs={{0,63},{1,2},{2,1},{3,4},{4,3},{5,6},{6,5},{7,8},{8,7},{9,10},{10,... | collective-permute-start | bytes 1179656 | tf_op jit(solution)/shard_map/ppermute | solution.py:427
  11.0 0.0 copy-start
  11.0 0.0 copy-start.1
  11.0 0.0 copy-start.2
  11.0 0.0 copy-start.3
  11.0 2.5 %forecast_inner.1.inner_ref = f32[3,16,32,512]{3,2,1,0:T(8,128)S(1)} custom-call(f32[3,1024,128]{2,1,0:T(8,128)S(1)} %get-tuple-element.26.x_ref), custom_call_target="tpu_custom_call" | custom-call | flops 19660800 | bytes 3145728 | tf_op jit(solution)/shard_map/forecast_inner/pallas_call | solution.py:135
  13.5 0.0 copy-done
  13.5 0.0 copy-done.1
  13.5 0.0 copy-done.2
  13.5 0.0 copy-done.3
  13.5 1.2 %slots_to_cells.1 = (f32[128,1024]{1,0:T(8,128)S(1)}, f32[8,1024]{1,0:T(8,128)S(1)}) custom-call(s32[1,1]{1,0:T(1,128)S(6)} %copy.7.count_ref, s32[1,1024]{1,0:T(1,128)S(1)} %bitcast.11, f32[1,1024]{1,0:T(1,128)S(1)} %bitcast.12, f32[1,1024]{1,0:T(1,128)S(1)} %bitcast.13, f32[1024,128]{1,0:T(8,128)S(1)} %bitcast.10), custom_call_target="tpu_custom_call" | custom-call | flops 536870912 | bytes 1048576 | tf_op jit(solution)/shard_map/slots_to_cells/pallas_call | solution.py:256
  14.7 0.0 collective-permute-done.halo_ref
  14.7 2.2 %forecast_first.1 = (bf16[3,4,32,128]{3,2,1,0:T(8,128)(2,1)S(1)}, bf16[3,4,32,128]{3,2,1,0:T(8,128)(2,1)S(1)}, bf16[3,4,32,128]{3,2,1,0:T(8,128)(2,1)S(1)}, bf16[3,4,32,128]{3,2,1,0:T(8,128)(2,1)S(1)}) custom-call(f32[3,16,32,512]{3,2,1,0:T(8,128)S(1)} %forecast_inner.1.inner_ref, bf16[3,4,32,512]{3,2,1,0:T(8,128)(2,1)S(1)} %collective-permute-done.halo_ref), custom_call_target="tpu_custom_call" | custom-call | flops 31457280 | bytes 3145728 | tf_op jit(solution)/shard_map/forecast_first/pallas_call | solution.py:200
  16.9 0.0 collective-permute-done.1.halo_ref
  16.9 2.4 %forecast_second.1 = (bf16[3,4,32,128]{3,2,1,0:T(8,128)(2,1)S(1)}, bf16[3,8,32,128]{3,2,1,0:T(8,128)(2,1)S(1)}, bf16[1,8,32,128]{3,2,1,0:T(8,128)(2,1)S(1)}, bf1...) custom-call(f32[3,16,32,512]{3,2,1,0:T(8,128)S(1)} %forecast_inner.1.inner, ...), custom_call_target="tpu_custom_call" | custom-call | flops 31457280 | bytes 3145728 | tf_op jit(solution)/shard_map/forecast_second/pallas_call | solution.py:200
  19.3 2.4 %collective-permute-start.2 = (bf16[3,8,32,128]{3,2,1,0:T(8,128)(2,1)S(1)}, bf16[3,8,32,128]{3,2,1,0:T(8,128)(2,1)S(1)}, u32[]{:S(2)}, u32[]{:S(2)}) collective-permute-start(bf16[3,8,32,128]{3,2,1,0:T(8,128)(2,1)S(1)} %get-tuple-element.40), channel_id=1, source_target_pairs={{0,128},{64,192},{128,0},{192,64},{1,129},{65,193},{129,1},{193,65... | collective-permute-start | bytes 589832 | tf_op jit(solution)/shard_map/ppermute | solution.py:416
  21.7 1.3 %collective-permute-start.3 = (bf16[1,8,32,128]{3,2,1,0:T(8,128)(2,1)S(1)}, bf16[1,8,32,128]{3,2,1,0:T(8,128)(2,1)S(1)}, u32[]{:S(2)}, u32[]{:S(2)}) collective-permute-start(bf16[1,8,32,128]{3,2,1,0:T(8,128)(2,1)S(1)} %get-tuple-element.41), channel_id=1, source_target_pairs={{0,64},{64,0},{128,192},{192,128},{1,65},{65,1},{129,193},{193,129... | collective-permute-start | bytes 196616 | tf_op jit(solution)/shard_map/ppermute | solution.py:416
  23.0 0.4 %collective-permute-start.4 = (bf16[1,8,32,128]{3,2,1,0:T(8,128)(2,1)S(1)}, bf16[1,8,32,128]{3,2,1,0:T(8,128)(2,1)S(1)}, u32[]{:S(2)}, u32[]{:S(2)}) collective-permute-start(bf16[1,8,32,128]{3,2,1,0:T(8,128)(2,1)S(1)} %get-tuple-element.42), channel_id=1, source_target_pairs={{0,192},{64,128},{128,64},{192,0},{1,193},{65,129},{129,65},{193,1... | collective-permute-start | bytes 196616 | tf_op jit(solution)/shard_map/ppermute | solution.py:416
  23.5 0.6 %collective-permute-start.5 = (bf16[2,8,32,128]{3,2,1,0:T(8,128)(2,1)S(1)}, bf16[2,8,32,128]{3,2,1,0:T(8,128)(2,1)S(1)}, u32[]{:S(2)}, u32[]{:S(2)}) collective-permute-start(bf16[2,8,32,128]{3,2,1,0:T(8,128)(2,1)S(1)} %get-tuple-element.43), channel_id=1, source_target_pairs={{0,64},{64,0},{128,192},{192,128},{1,65},{65,1},{129,193},{193,129... | collective-permute-start | bytes 393224 | tf_op jit(solution)/shard_map/ppermute | solution.py:416
  24.1 2.3 %collective-permute-start.6 = (bf16[2,8,32,128]{3,2,1,0:T(8,128)(2,1)S(1)}, bf16[2,8,32,128]{3,2,1,0:T(8,128)(2,1)S(1)}, u32[]{:S(2)}, u32[]{:S(2)}) collective-permute-start(bf16[2,8,32,128]{3,2,1,0:T(8,128)(2,1)S(1)} %get-tuple-element.44), channel_id=1, source_target_pairs={{0,192},{64,128},{128,64},{192,0},{1,193},{65,129},{129,65},{193,1... | collective-permute-start | bytes 393224 | tf_op jit(solution)/shard_map/ppermute | solution.py:416
  26.3 3.8 %collective-permute-done.3.refs_3_ = bf16[1,8,32,128]{3,2,1,0:T(8,128)(2,1)S(1)} collective-permute-done((bf16[1,8,32,128]{3,2,1,0:T(8,128)(2,1)S(1)}, bf16[1,8,32,128]{3,2,1,0:T(8,128)(2,1)S(1)}, u32[]{:S(2)}, u32[]{:S(2)}) %collective-permute-start.3) | collective-permute-done | bytes 65568 | tf_op jit(solution)/shard_map/ppermute | solution.py:416
  30.2 0.0 collective-permute-done.4.refs_4_
  30.2 0.0 collective-permute-done.2.refs_2_
  30.2 2.7 %weights.1.w_ref = bf16[128,256]{1,0:T(8,128)(2,1)S(1)} custom-call(f32[128,1024]{1,0:T(8,128)S(1)} %get-tuple-element.30.z_ref, f32[8,1024]{1,0:T(8,128)S(1)} %get-tuple-element.31.omega_ref, bf16[3,4,32,128]{3,2,1,0:T(8,128)(2,1)S(1)} %get-tuple-element.34.refs_0_, bf16[3,4,32,128]{3,2,1,0:T(8,128)(2,1)S(1)} %get-tuple-element.39.refs_1_, ...), custom_call_target="tpu_custom_call" | custom-call | flops 8388608000 | bytes 1048576 | tf_op jit(solution)/shard_map/weights/pallas_call | solution.py:350
  32.9 0.0 collective-permute-done.5.refs_5_
  32.9 0.0 collective-permute-done.6.refs_6_
  32.9 1.4 %apply_weights.1 = bf16[3,1024,128]{2,1,0:T(8,128)(2,1)} custom-call(bf16[128,256]{1,0:T(8,128)(2,1)S(1)} %weights.1.w_ref, bf16[3,4,32,128]{3,2,1,0:T(8,128)(2,1)S(1)} %get-tuple-element.34.refs_0_, bf16[3,4,32,128]{3,2,1,0:T(8,128)(2,1)S(1)} %get-tuple-element.39.refs_1_, bf16[3,8,32,128]{3,2,1,0:T(8,128)(2,1)S(1)} %collective-permute-done.2.refs_2_, ...), custom_call_target="tpu_custom_call" | custom-call | flops 201326592 | bytes 1572864 | tf_op jit(solution)/shard_map/apply_weights/pallas_call | solution.py:396
Async XLA Ops:
  2.0 12.7 %collective-permute-start = (bf16[3,4,32,512]{3,2,1,0:T(8,128)(2,1)S(1)}, bf16[3,4,32,512]{3,2,1,0:T(8,128)(2,1)S(1)}, u32[]{:S(2)}, u32[]{:S(2)}) collective-permute-start(bf16[3,4,32,512]{3,2,1,0:T(8,128)(2,1)S(1)} %get-tuple-element.25), channel_id=1, source_target_pairs={{0,1},{1,0},{2,3},{3,2},{4,5},{5,4},{6,7},{7,6},{8,9},{9,8},{10,11... | collective-permute-start | bytes 1179656 | tf_op jit(solution)/shard_map/ppermute | solution.py:426
  4.0 12.9 %collective-permute-start.1 = (bf16[3,4,32,512]{3,2,1,0:T(8,128)(2,1)S(1)}, bf16[3,4,32,512]{3,2,1,0:T(8,128)(2,1)S(1)}, u32[]{:S(2)}, u32[]{:S(2)}) collective-permute-start(bf16[3,4,32,512]{3,2,1,0:T(8,128)(2,1)S(1)} %get-tuple-element.35), channel_id=1, source_target_pairs={{0,63},{1,2},{2,1},{3,4},{4,3},{5,6},{6,5},{7,8},{8,7},{9,10},{10,... | collective-permute-start | bytes 1179656 | tf_op jit(solution)/shard_map/ppermute | solution.py:427
  11.0 2.5 %copy-start = (f32[1,1,1024,128]{3,2,1,0:T(8,128)S(1)}, f32[1,1,1024,128]{3,2,1,0:T(8,128)}, u32[]{:S(2)}) copy-start(f32[1,1,1024,128]{3,2,1,0:T(8,128)} %param.11) | copy-start | bytes 1572868
  11.0 2.5 %copy-start.1 = (s32[1,1,1024]{2,1,0:T(1,128)S(1)}, s32[1,1,1024]{2,1,0:T(1,128)}, u32[]{:S(2)}) copy-start(s32[1,1,1024]{2,1,0:T(1,128)} %param.7) | copy-start | bytes 12292
  11.0 2.5 %copy-start.2 = (f32[1,1,1024]{2,1,0:T(1,128)S(1)}, f32[1,1,1024]{2,1,0:T(1,128)}, u32[]{:S(2)}) copy-start(f32[1,1,1024]{2,1,0:T(1,128)} %param.9) | copy-start | bytes 12292
  11.0 2.5 %copy-start.3 = (f32[1,1,1024]{2,1,0:T(1,128)S(1)}, f32[1,1,1024]{2,1,0:T(1,128)}, u32[]{:S(2)}) copy-start(f32[1,1,1024]{2,1,0:T(1,128)} %param.10) | copy-start | bytes 12292
  19.3 10.9 %collective-permute-start.2 = (bf16[3,8,32,128]{3,2,1,0:T(8,128)(2,1)S(1)}, bf16[3,8,32,128]{3,2,1,0:T(8,128)(2,1)S(1)}, u32[]{:S(2)}, u32[]{:S(2)}) collective-permute-start(bf16[3,8,32,128]{3,2,1,0:T(8,128)(2,1)S(1)} %get-tuple-element.40), channel_id=1, source_target_pairs={{0,128},{64,192},{128,0},{192,64},{1,129},{65,193},{129,1},{193,65... | collective-permute-start | bytes 589832 | tf_op jit(solution)/shard_map/ppermute | solution.py:416
  21.7 8.5 %collective-permute-start.3 = (bf16[1,8,32,128]{3,2,1,0:T(8,128)(2,1)S(1)}, bf16[1,8,32,128]{3,2,1,0:T(8,128)(2,1)S(1)}, u32[]{:S(2)}, u32[]{:S(2)}) collective-permute-start(bf16[1,8,32,128]{3,2,1,0:T(8,128)(2,1)S(1)} %get-tuple-element.41), channel_id=1, source_target_pairs={{0,64},{64,0},{128,192},{192,128},{1,65},{65,1},{129,193},{193,129... | collective-permute-start | bytes 196616 | tf_op jit(solution)/shard_map/ppermute | solution.py:416
  23.0 7.2 %collective-permute-start.4 = (bf16[1,8,32,128]{3,2,1,0:T(8,128)(2,1)S(1)}, bf16[1,8,32,128]{3,2,1,0:T(8,128)(2,1)S(1)}, u32[]{:S(2)}, u32[]{:S(2)}) collective-permute-start(bf16[1,8,32,128]{3,2,1,0:T(8,128)(2,1)S(1)} %get-tuple-element.42), channel_id=1, source_target_pairs={{0,192},{64,128},{128,64},{192,0},{1,193},{65,129},{129,65},{193,1... | collective-permute-start | bytes 196616 | tf_op jit(solution)/shard_map/ppermute | solution.py:416
  23.5 9.4 %collective-permute-start.5 = (bf16[2,8,32,128]{3,2,1,0:T(8,128)(2,1)S(1)}, bf16[2,8,32,128]{3,2,1,0:T(8,128)(2,1)S(1)}, u32[]{:S(2)}, u32[]{:S(2)}) collective-permute-start(bf16[2,8,32,128]{3,2,1,0:T(8,128)(2,1)S(1)} %get-tuple-element.43), channel_id=1, source_target_pairs={{0,64},{64,0},{128,192},{192,128},{1,65},{65,1},{129,193},{193,129... | collective-permute-start | bytes 393224 | tf_op jit(solution)/shard_map/ppermute | solution.py:416
  24.1 8.8 %collective-permute-start.6 = (bf16[2,8,32,128]{3,2,1,0:T(8,128)(2,1)S(1)}, bf16[2,8,32,128]{3,2,1,0:T(8,128)(2,1)S(1)}, u32[]{:S(2)}, u32[]{:S(2)}) collective-permute-start(bf16[2,8,32,128]{3,2,1,0:T(8,128)(2,1)S(1)} %get-tuple-element.44), channel_id=1, source_target_pairs={{0,192},{64,128},{128,64},{192,0},{1,193},{65,129},{129,65},{193,1... | collective-permute-start | bytes 393224 | tf_op jit(solution)/shard_map/ppermute | solution.py:416

commit v3 on v2

--- a/solution.py
+++ b/solution.py
@@ -26,29 +26,35 @@
     )
 
 
-def edges_kernel(x_hbm, x_ref, first_ref, second_ref, sems):
+def edges_kernel(x_hbm, x_ref, first_ref, *refs):
+    seconds, sems = refs[:-1], refs[-1]
     members, cols = first_ref.shape[2:]
+    part = members // len(seconds)
+    outs = [(first_ref, 0, 0)] + [(ref, 1, k * part) for k, ref in enumerate(seconds)]
     odd = lax.axis_index("grp")
     copies = [pltpu.make_async_copy(x_hbm.at[f], x_ref.at[f], sems.at[f]) for f in range(3)]
     for copy in copies:
         copy.start()
     for f in range(3):
         copies[f].wait()
-        for out_ref, base in ((first_ref, STEPS * (1 - odd)), (second_ref, STEPS * odd)):
+        for out_ref, beyond, begin in outs:
+            base = STEPS * odd if beyond else STEPS * (1 - odd)
             for r in range(STEPS):
                 for t in range(cols // 128):
-                    q = x_ref[f, pl.ds(base + (t * 8 + r), members, stride=cols // 16), :]
+                    at = base + (begin * (cols // 16) + t * 8 + r)
+                    q = x_ref[f, pl.ds(at, out_ref.shape[2], stride=cols // 16), :]
                     out_ref[f, r, :, pl.ds(t * 128, 128)] = q.astype(BF16)
 
 
 def edges(x, cols):
     members = x.shape[1] * 16 // cols
     shape = jax.ShapeDtypeStruct((3, STEPS, members, cols), BF16)
+    half = jax.ShapeDtypeStruct((3, STEPS, members // 2, cols), BF16)
     return pl.pallas_call(
         edges_kernel,
         in_specs=[pl.BlockSpec(memory_space=pltpu.HBM)],
-        out_specs=[pl.BlockSpec(memory_space=pltpu.VMEM)] * 3,
-        out_shape=[jax.ShapeDtypeStruct(x.shape, F32), shape, shape],
+        out_specs=[pl.BlockSpec(memory_space=pltpu.VMEM)] * 4,
+        out_shape=[jax.ShapeDtypeStruct(x.shape, F32), shape, half, half],
         scratch_shapes=[pltpu.SemaphoreType.DMA((3,))],
         compiler_params=pltpu.CompilerParams(vmem_limit_bytes=16 * MIB),
         cost_estimate=pl.CostEstimate(flops=x.size, bytes_accessed=x.size * 6, transcendentals=0),
@@ -143,9 +149,12 @@
     )(x)
 
 
-def side_kernel(second, plan, tiles, inner_ref, halo_ref, *refs):
-    outs, (ping, pong, edge) = refs[-3 - len(plan) : -3], refs[-3:]
-    before = refs[: -3 - len(plan)]
+def side_kernel(second, plan, tiles, begin, inner_ref, halo_ref, *refs):
+    count = max(1, len(plan))
+    outs, (ping, pong, edge) = refs[-3 - count : -3], refs[-3:]
+    before = refs[: -3 - count]
+    if begin:
+        before, other = before[:-1], before[-1]
     members, cols = halo_ref.shape[2:]
     for f in range(3):
         for r in range(STEPS):
@@ -158,12 +167,13 @@
 
         def group(g, _):
             part = pl.ds(pl.multiple_of(g * 8, 8), 8)
+            held = pl.ds(pl.multiple_of(begin + g * 8, 8), 8)
             for step in range(1, STEPS + 1):
                 source_ref, target_ref = (ping, pong) if step % 2 else (pong, ping)
 
                 def source(f, p):
                     if step - 1 <= p < 9 - step:
-                        return inner_ref[f, INNER.index((step - 1, p)), part, :]
+                        return inner_ref[f, INNER.index((step - 1, p)), held, :]
                     if step == 1:
                         return edge[f, p - 8 if above else p + STEPS, part, :]
                     return source_ref[f, p - first_row(step - 1), part, :]
@@ -180,6 +190,10 @@
     pl.when(from_above)(lambda: side(True))
     pl.when(jnp.logical_not(from_above))(lambda: side(False))
     last = ping if STEPS % 2 == 0 else pong
+    if not plan:
+        outs[0][...] = last[...]
+        return
+    sources = [(last, pl.ds(begin, members))] + ([(other, pl.ds(0, begin))] if begin else [])
     rank = lax.axis_index("mem")
     for (shift, fields), out_ref in zip(plan, outs):
         base = out_ref.shape[1] - STEPS
@@ -188,23 +202,25 @@
             if base:
                 out_ref[k, :STEPS] = before[shift][f]
             for r in range(STEPS):
-                q = last[f, r, :, part]
-                q = q * (1.0 / CH) - 1.0 if f == 0 else q * (1.0 / CU)
-                out_ref[k, base + r] = q.astype(BF16)
-
-
-def side_part(inner, halo, second, plan, tiles, before=()):
+                for ref, place in sources:
+                    q = ref[f, r, :, part]
+                    q = q * (1.0 / CH) - 1.0 if f == 0 else q * (1.0 / CU)
+                    out_ref[k, base + r, place, :] = q.astype(BF16)
+
+
+def side_part(inner, halo, second, plan, tiles, before=(), begin=0):
     members, cols = halo.shape[2:]
     vmem = pl.BlockSpec(memory_space=pltpu.VMEM)
     rows = [STEPS if shift == 0 or not second else 2 * STEPS for shift, _ in plan]
     return pl.pallas_call(
-        functools.partial(side_kernel, second, plan, tiles),
+        functools.partial(side_kernel, second, plan, tiles, begin),
         in_specs=[vmem] * (2 + len(before)),
-        out_specs=[vmem] * len(plan),
+        out_specs=[vmem] * max(1, len(plan)),
         out_shape=[
-            jax.ShapeDtypeStruct((len(fields), n, members, 128), BF16)
+            jax.ShapeDtypeStruct((len(fields), n, begin + members, 128), BF16)
             for n, (_, fields) in zip(rows, plan)
-        ],
+        ]
+        or [jax.ShapeDtypeStruct((3, STEPS, members, cols), F32)],
         scratch_shapes=[pltpu.VMEM((3, STEPS, members, cols), F32)] * 3,
         compiler_params=pltpu.CompilerParams(vmem_limit_bytes=24 * MIB),
         cost_estimate=pl.CostEstimate(
@@ -420,11 +436,11 @@
     fields, count, lines, cols = members.shape
     x = members.reshape(fields, count, lines, cols // 128, 128)
     x = x.transpose(0, 1, 3, 2, 4).reshape(fields, -1, 128)
-    x, first, second = edges(x, cols)
+    x, first, *seconds = edges(x, cols)
     slabs = lax.axis_size("tile") * lax.axis_size("grp")
     beyond = [(s, (s + 1 if s % 2 else s - 1) % slabs) for s in range(slabs)]
     halo_first = lax.ppermute(first, "grp", [(0, 1), (1, 0)])
-    halo_second = lax.ppermute(second, ("tile", "grp"), beyond)
+    halo_seconds = [lax.ppermute(second, ("tile", "grp"), beyond) for second in seconds]
     inner = inner_part(x, cols)
     slots = obs_cells.shape[-1]
     obs_count, inner = lax.optimization_barrier((obs_count, inner))
@@ -442,7 +458,10 @@
     far = size // 2
     near = [s for s in range(1, size) if s != far]
     plan = [(0, every), (far, every)] + [(s, (0,)) for s in near] + [(s, every[1:]) for s in near]
-    late = side_part(inner, halo_second, True, tuple(plan), size, early)
+    half = count // 2
+    halo_seconds[0], early = lax.optimization_barrier((halo_seconds[0], early))
+    (rows,) = side_part(inner, halo_seconds[0], True, (), size)
+    late = side_part(inner, halo_seconds[1], True, tuple(plan), size, [*early, rows], half)
     arrays = [early[0]]
     where = [[None] * fields for _ in range(size)]
     for k, ((shift, held), block) in enumerate(zip(plan, late)):

time: 34.5 us -> 34.2 us (level)
    ppermute x5, waiting for transfers between devices: 3.86 us -> 3.03 us  [send(): return lax.ppermute(x, 'mem', [(i, i ^ shift) for i in range(size)])]
    ppermute x1 -> x2, waiting for transfers between devices: 0.01 us -> 0.62 us  [body(): lax.ppermute(second, ('tile', 'grp'), beyond)]
    ppermute x1 -> x2, starting transfers between devices: 6.3 us -> 6.33 us  [body(): lax.ppermute(second, ('tile', 'grp'), beyond)]
    pallas_call x2 -> x3, Pallas kernels: 4.58 us -> 4.6 us  [side_part(): pl.pallas_call(functools.partial(side_kernel, second, plan, tiles, begin)...]
  transfers between devices with their start and end apart: 7 -> 8, of which waited for: 1 -> 2; matrix products, arithmetic and copies ran while one was open for 0% -> 0% of each run, Pallas kernels for 25% -> 28%
where the time goes in v3:
time: 34.2 us; the launch traced here: 34.1 us
  starting transfers between devices  15.4 us (45%)
  Pallas kernels  14.2 us (42%)
  waiting for transfers between devices  3.65 us (11%)
  between operations  0.81 us (2%)
    ppermute x5, starting transfers between devices, send(): return lax.ppermute(x, 'mem', [(i, i ^ shift) for i in range(size)])  7.04 us
    ppermute x2, starting transfers between devices, body(): lax.ppermute(second, ('tile', 'grp'), beyond)  6.33 us
    pallas_call x3, Pallas kernels, side_part(): pl.pallas_call(functools.partial(side_kernel, second, plan, tiles, begin)...  4.6 us
    ppermute x5, waiting for transfers between devices, send(): return lax.ppermute(x, 'mem', [(i, i ^ shift) for i in range(size)])  3.03 us
    pallas_call x1, Pallas kernels, weights(): pl.pallas_call(functools.partial(weights_kernel, where), in_specs=[vmem]...  2.67 us
    pallas_call x1, Pallas kernels, inner_part(): pl.pallas_call(inner_kernel, in_specs=[vmem], out_specs=vmem, out_shape=j...  2.47 us
    ppermute x1, starting transfers between devices, body(): halo_first = lax.ppermute(first, 'grp', [(0, 1), (1, 0)])  2 us
    pallas_call x1, Pallas kernels, edges(): pl.pallas_call(edges_kernel, in_specs=[pl.BlockSpec(memory_space=pltpu.HB...  1.99 us
  transfers between devices with their start and end apart: 8, of which 2 were waited for; matrix products, arithmetic and copies ran while one was open for 0% of the time, Pallas kernels for 28%

profile of v3, /device:TPU:8, one launch (start us, length us, event | category | flops | bytes accessed | tf_op | source)
XLA Modules:
  0.0 34.1 jit_solution(9910166957395744152)
XLA Ops:
  0.0 2.0 %edges.1 = (f32[3,1024,128]{2,1,0:T(8,128)S(1)}, bf16[3,4,32,512]{3,2,1,0:T(8,128)(2,1)S(1)}, bf16[3,4,16,512]{3,2,1,0:T(8,128)(2,1)S(1)}, bf16[3,4,16,512]{3,2,1,0:T(8,128)(2,1)S(1)}) custom-call(f32[3,1024,128]{2,1,0:T(8,128)} %bitcast.14), custom_call_target="tpu_custom_call" | custom-call | flops 393216 | bytes 2359296 | tf_op jit(solution)/shard_map/edges/pallas_call | solution.py:53
  2.0 2.0 %collective-permute-start = (bf16[3,4,32,512]{3,2,1,0:T(8,128)(2,1)S(1)}, bf16[3,4,32,512]{3,2,1,0:T(8,128)(2,1)S(1)}, u32[]{:S(2)}, u32[]{:S(2)}) collective-permute-start(bf16[3,4,32,512]{3,2,1,0:T(8,128)(2,1)S(1)} %get-tuple-element.31), channel_id=1, source_target_pairs={{0,1},{1,0},{2,3},{3,2},{4,5},{5,4},{6,7},{7,6},{8,9},{9,8},{10,11... | collective-permute-start | bytes 1179656 | tf_op jit(solution)/shard_map/ppermute | solution.py:442
  4.0 6.3 %collective-permute-start.1 = (bf16[3,4,16,512]{3,2,1,0:T(8,128)(2,1)S(1)}, bf16[3,4,16,512]{3,2,1,0:T(8,128)(2,1)S(1)}, u32[]{:S(2)}, u32[]{:S(2)}) collective-permute-start(bf16[3,4,16,512]{3,2,1,0:T(8,128)(2,1)S(1)} %get-tuple-element.38), channel_id=1, source_target_pairs={{0,63},{1,2},{2,1},{3,4},{4,3},{5,6},{6,5},{7,8},{8,7},{9,10},{10,... | collective-permute-start | bytes 589832 | tf_op jit(solution)/shard_map/ppermute | solution.py:443
  10.3 0.0 collective-permute-start.2
  11.0 0.0 copy-start
  11.0 0.0 copy-start.1
  11.0 0.0 copy-start.2
  11.0 0.0 copy-start.3
  11.0 2.5 %forecast_inner.1.inner_ref = f32[3,16,32,512]{3,2,1,0:T(8,128)S(1)} custom-call(f32[3,1024,128]{2,1,0:T(8,128)S(1)} %get-tuple-element.32.x_ref), custom_call_target="tpu_custom_call" | custom-call | flops 19660800 | bytes 3145728 | tf_op jit(solution)/shard_map/forecast_inner/pallas_call | solution.py:141
  13.5 0.0 copy-done
  13.5 0.0 copy-done.1
  13.5 0.0 copy-done.2
  13.5 0.0 copy-done.3
  13.6 1.2 %slots_to_cells.1 = (f32[128,1024]{1,0:T(8,128)S(1)}, f32[8,1024]{1,0:T(8,128)S(1)}) custom-call(s32[1,1]{1,0:T(1,128)S(6)} %copy.7.count_ref, s32[1,1024]{1,0:T(1,128)S(1)} %bitcast.11, f32[1,1024]{1,0:T(1,128)S(1)} %bitcast.12, f32[1,1024]{1,0:T(1,128)S(1)} %bitcast.13, f32[1024,128]{1,0:T(8,128)S(1)} %bitcast.10), custom_call_target="tpu_custom_call" | custom-call | flops 536870912 | bytes 1048576 | tf_op jit(solution)/shard_map/slots_to_cells/pallas_call | solution.py:272
  14.7 0.0 collective-permute-done.halo_ref
  14.7 2.2 %forecast_first.1 = (bf16[3,4,32,128]{3,2,1,0:T(8,128)(2,1)S(1)}, bf16[3,4,32,128]{3,2,1,0:T(8,128)(2,1)S(1)}, bf16[3,4,32,128]{3,2,1,0:T(8,128)(2,1)S(1)}, bf16[3,4,32,128]{3,2,1,0:T(8,128)(2,1)S(1)}) custom-call(f32[3,16,32,512]{3,2,1,0:T(8,128)S(1)} %forecast_inner.1.inner_ref, bf16[3,4,32,512]{3,2,1,0:T(8,128)(2,1)S(1)} %collective-permute-done.halo_ref), custom_call_target="tpu_custom_call" | custom-call | flops 31457280 | bytes 3145728 | tf_op jit(solution)/shard_map/forecast_first/pallas_call | solution.py:215
  16.9 0.0 collective-permute-done.1.halo_ref
  16.9 1.2 %forecast_second.2.refs_4_ = f32[3,4,16,512]{3,2,1,0:T(8,128)S(1)} custom-call(f32[3,16,32,512]{3,2,1,0:T(8,128)S(1)} %forecast_inner.1.inner_ref, bf16[3,4,16,512]{3,2,1,0:T(8,128)(2,1)S(1)} %collective-permute-done.1.halo_ref), custom_call_target="tpu_custom_call" | custom-call | flops 15728640 | bytes 1572864 | tf_op jit(solution)/shard_map/forecast_second/pallas_call | solution.py:215
  18.1 0.6 %collective-permute-done.2.halo_ref = bf16[3,4,16,512]{3,2,1,0:T(8,128)(2,1)S(1)} collective-permute-done((bf16[3,4,16,512]{3,2,1,0:T(8,128)(2,1)S(1)}, bf16[3,4,16,512]{3,2,1,0:T(8,128)(2,1)S(1)}, u32[]{:S(2)}, u32[]{:S(2)}) %collective-permute-start.2) | collective-permute-done | bytes 196640 | tf_op jit(solution)/shard_map/ppermute | solution.py:443
  18.7 1.2 %forecast_second.3 = (bf16[3,4,32,128]{3,2,1,0:T(8,128)(2,1)S(1)}, bf16[3,8,32,128]{3,2,1,0:T(8,128)(2,1)S(1)}, bf16[1,8,32,128]{3,2,1,0:T(8,128)(2,1)S(1)}, bf1...) custom-call(f32[3,16,32,512]{3,2,1,0:T(8,128)S(1)} %forecast_inner.1.inner, ...), custom_call_target="tpu_custom_call" | custom-call | flops 15728640 | bytes 1572864 | tf_op jit(solution)/shard_map/forecast_second/pallas_call | solution.py:215
  20.0 2.4 %collective-permute-start.3 = (bf16[3,8,32,128]{3,2,1,0:T(8,128)(2,1)S(1)}, bf16[3,8,32,128]{3,2,1,0:T(8,128)(2,1)S(1)}, u32[]{:S(2)}, u32[]{:S(2)}) collective-permute-start(bf16[3,8,32,128]{3,2,1,0:T(8,128)(2,1)S(1)} %get-tuple-element.52), channel_id=1, source_target_pairs={{0,128},{64,192},{128,0},{192,64},{1,129},{65,193},{129,1},{193,65... | collective-permute-start | bytes 589832 | tf_op jit(solution)/shard_map/ppermute | solution.py:432
  22.4 1.3 %collective-permute-start.4 = (bf16[1,8,32,128]{3,2,1,0:T(8,128)(2,1)S(1)}, bf16[1,8,32,128]{3,2,1,0:T(8,128)(2,1)S(1)}, u32[]{:S(2)}, u32[]{:S(2)}) collective-permute-start(bf16[1,8,32,128]{3,2,1,0:T(8,128)(2,1)S(1)} %get-tuple-element.53), channel_id=1, source_target_pairs={{0,64},{64,0},{128,192},{192,128},{1,65},{65,1},{129,193},{193,129... | collective-permute-start | bytes 196616 | tf_op jit(solution)/shard_map/ppermute | solution.py:432
  23.7 0.4 %collective-permute-start.5 = (bf16[1,8,32,128]{3,2,1,0:T(8,128)(2,1)S(1)}, bf16[1,8,32,128]{3,2,1,0:T(8,128)(2,1)S(1)}, u32[]{:S(2)}, u32[]{:S(2)}) collective-permute-start(bf16[1,8,32,128]{3,2,1,0:T(8,128)(2,1)S(1)} %get-tuple-element.54), channel_id=1, source_target_pairs={{0,192},{64,128},{128,64},{192,0},{1,193},{65,129},{129,65},{193,1... | collective-permute-start | bytes 196616 | tf_op jit(solution)/shard_map/ppermute | solution.py:432
  24.2 0.6 %collective-permute-start.6 = (bf16[2,8,32,128]{3,2,1,0:T(8,128)(2,1)S(1)}, bf16[2,8,32,128]{3,2,1,0:T(8,128)(2,1)S(1)}, u32[]{:S(2)}, u32[]{:S(2)}) collective-permute-start(bf16[2,8,32,128]{3,2,1,0:T(8,128)(2,1)S(1)} %get-tuple-element.55), channel_id=1, source_target_pairs={{0,64},{64,0},{128,192},{192,128},{1,65},{65,1},{129,193},{193,129... | collective-permute-start | bytes 393224 | tf_op jit(solution)/shard_map/ppermute | solution.py:432
  24.8 2.3 %collective-permute-start.7 = (bf16[2,8,32,128]{3,2,1,0:T(8,128)(2,1)S(1)}, bf16[2,8,32,128]{3,2,1,0:T(8,128)(2,1)S(1)}, u32[]{:S(2)}, u32[]{:S(2)}) collective-permute-start(bf16[2,8,32,128]{3,2,1,0:T(8,128)(2,1)S(1)} %get-tuple-element.56), channel_id=1, source_target_pairs={{0,192},{64,128},{128,64},{192,0},{1,193},{65,129},{129,65},{193,1... | collective-permute-start | bytes 393224 | tf_op jit(solution)/shard_map/ppermute | solution.py:432
  27.0 3.0 %collective-permute-done.4.refs_3_ = bf16[1,8,32,128]{3,2,1,0:T(8,128)(2,1)S(1)} collective-permute-done((bf16[1,8,32,128]{3,2,1,0:T(8,128)(2,1)S(1)}, bf16[1,8,32,128]{3,2,1,0:T(8,128)(2,1)S(1)}, u32[]{:S(2)}, u32[]{:S(2)}) %collective-permute-start.4) | collective-permute-done | bytes 65568 | tf_op jit(solution)/shard_map/ppermute | solution.py:432
  30.0 0.0 collective-permute-done.5.refs_4_
  30.0 0.0 collective-permute-done.3.refs_2_
  30.0 2.7 %weights.1.w_ref = bf16[128,256]{1,0:T(8,128)(2,1)S(1)} custom-call(f32[128,1024]{1,0:T(8,128)S(1)} %get-tuple-element.36.z_ref, f32[8,1024]{1,0:T(8,128)S(1)} %get-tuple-element.37.omega_ref, bf16[3,4,32,128]{3,2,1,0:T(8,128)(2,1)S(1)} %get-tuple-element.45.refs_0_, bf16[3,4,32,128]{3,2,1,0:T(8,128)(2,1)S(1)} %get-tuple-element.51.refs_1_, ...), custom_call_target="tpu_custom_call" | custom-call | flops 8388608000 | bytes 1048576 | tf_op jit(solution)/shard_map/weights/pallas_call | solution.py:366
  32.7 0.0 collective-permute-done.6.refs_5_
  32.7 0.0 collective-permute-done.7.refs_6_
  32.7 1.4 %apply_weights.1 = bf16[3,1024,128]{2,1,0:T(8,128)(2,1)} custom-call(bf16[128,256]{1,0:T(8,128)(2,1)S(1)} %weights.1.w_ref, bf16[3,4,32,128]{3,2,1,0:T(8,128)(2,1)S(1)} %get-tuple-element.45.refs_0_, bf16[3,4,32,128]{3,2,1,0:T(8,128)(2,1)S(1)} %get-tuple-element.51.refs_1_, bf16[3,8,32,128]{3,2,1,0:T(8,128)(2,1)S(1)} %collective-permute-done.3.refs_2_, ...), custom_call_target="tpu_custom_call" | custom-call | flops 201326592 | bytes 1572864 | tf_op jit(solution)/shard_map/apply_weights/pallas_call | solution.py:412
Async XLA Ops:
  2.0 12.7 %collective-permute-start = (bf16[3,4,32,512]{3,2,1,0:T(8,128)(2,1)S(1)}, bf16[3,4,32,512]{3,2,1,0:T(8,128)(2,1)S(1)}, u32[]{:S(2)}, u32[]{:S(2)}) collective-permute-start(bf16[3,4,32,512]{3,2,1,0:T(8,128)(2,1)S(1)} %get-tuple-element.31), channel_id=1, source_target_pairs={{0,1},{1,0},{2,3},{3,2},{4,5},{5,4},{6,7},{7,6},{8,9},{9,8},{10,11... | collective-permute-start | bytes 1179656 | tf_op jit(solution)/shard_map/ppermute | solution.py:442
  4.0 12.9 %collective-permute-start.1 = (bf16[3,4,16,512]{3,2,1,0:T(8,128)(2,1)S(1)}, bf16[3,4,16,512]{3,2,1,0:T(8,128)(2,1)S(1)}, u32[]{:S(2)}, u32[]{:S(2)}) collective-permute-start(bf16[3,4,16,512]{3,2,1,0:T(8,128)(2,1)S(1)} %get-tuple-element.38), channel_id=1, source_target_pairs={{0,63},{1,2},{2,1},{3,4},{4,3},{5,6},{6,5},{7,8},{8,7},{9,10},{10,... | collective-permute-start | bytes 589832 | tf_op jit(solution)/shard_map/ppermute | solution.py:443
  10.3 8.4 %collective-permute-start.2 = (bf16[3,4,16,512]{3,2,1,0:T(8,128)(2,1)S(1)}, bf16[3,4,16,512]{3,2,1,0:T(8,128)(2,1)S(1)}, u32[]{:S(2)}, u32[]{:S(2)}) collective-permute-start(bf16[3,4,16,512]{3,2,1,0:T(8,128)(2,1)S(1)} %get-tuple-element.46), channel_id=1, source_target_pairs={{0,63},{1,2},{2,1},{3,4},{4,3},{5,6},{6,5},{7,8},{8,7},{9,10},{10,... | collective-permute-start | bytes 589832 | tf_op jit(solution)/shard_map/ppermute | solution.py:443
  11.0 2.5 %copy-start = (f32[1,1,1024,128]{3,2,1,0:T(8,128)S(1)}, f32[1,1,1024,128]{3,2,1,0:T(8,128)}, u32[]{:S(2)}) copy-start(f32[1,1,1024,128]{3,2,1,0:T(8,128)} %param.11) | copy-start | bytes 1572868
  11.0 2.5 %copy-start.1 = (s32[1,1,1024]{2,1,0:T(1,128)S(1)}, s32[1,1,1024]{2,1,0:T(1,128)}, u32[]{:S(2)}) copy-start(s32[1,1,1024]{2,1,0:T(1,128)} %param.7) | copy-start | bytes 12292
  11.0 2.5 %copy-start.2 = (f32[1,1,1024]{2,1,0:T(1,128)S(1)}, f32[1,1,1024]{2,1,0:T(1,128)}, u32[]{:S(2)}) copy-start(f32[1,1,1024]{2,1,0:T(1,128)} %param.9) | copy-start | bytes 12292
  11.0 2.5 %copy-start.3 = (f32[1,1,1024]{2,1,0:T(1,128)S(1)}, f32[1,1,1024]{2,1,0:T(1,128)}, u32[]{:S(2)}) copy-start(f32[1,1,1024]{2,1,0:T(1,128)} %param.10) | copy-start | bytes 12292
  20.0 10.1 %collective-permute-start.3 = (bf16[3,8,32,128]{3,2,1,0:T(8,128)(2,1)S(1)}, bf16[3,8,32,128]{3,2,1,0:T(8,128)(2,1)S(1)}, u32[]{:S(2)}, u32[]{:S(2)}) collective-permute-start(bf16[3,8,32,128]{3,2,1,0:T(8,128)(2,1)S(1)} %get-tuple-element.52), channel_id=1, source_target_pairs={{0,128},{64,192},{128,0},{192,64},{1,129},{65,193},{129,1},{193,65... | collective-permute-start | bytes 589832 | tf_op jit(solution)/shard_map/ppermute | solution.py:432
  22.4 7.7 %collective-permute-start.4 = (bf16[1,8,32,128]{3,2,1,0:T(8,128)(2,1)S(1)}, bf16[1,8,32,128]{3,2,1,0:T(8,128)(2,1)S(1)}, u32[]{:S(2)}, u32[]{:S(2)}) collective-permute-start(bf16[1,8,32,128]{3,2,1,0:T(8,128)(2,1)S(1)} %get-tuple-element.53), channel_id=1, source_target_pairs={{0,64},{64,0},{128,192},{192,128},{1,65},{65,1},{129,193},{193,129... | collective-permute-start | bytes 196616 | tf_op jit(solution)/shard_map/ppermute | solution.py:432
  23.7 6.3 %collective-permute-start.5 = (bf16[1,8,32,128]{3,2,1,0:T(8,128)(2,1)S(1)}, bf16[1,8,32,128]{3,2,1,0:T(8,128)(2,1)S(1)}, u32[]{:S(2)}, u32[]{:S(2)}) collective-permute-start(bf16[1,8,32,128]{3,2,1,0:T(8,128)(2,1)S(1)} %get-tuple-element.54), channel_id=1, source_target_pairs={{0,192},{64,128},{128,64},{192,0},{1,193},{65,129},{129,65},{193,1... | collective-permute-start | bytes 196616 | tf_op jit(solution)/shard_map/ppermute | solution.py:432
  24.2 8.6 %collective-permute-start.6 = (bf16[2,8,32,128]{3,2,1,0:T(8,128)(2,1)S(1)}, bf16[2,8,32,128]{3,2,1,0:T(8,128)(2,1)S(1)}, u32[]{:S(2)}, u32[]{:S(2)}) collective-permute-start(bf16[2,8,32,128]{3,2,1,0:T(8,128)(2,1)S(1)} %get-tuple-element.55), channel_id=1, source_target_pairs={{0,64},{64,0},{128,192},{192,128},{1,65},{65,1},{129,193},{193,129... | collective-permute-start | bytes 393224 | tf_op jit(solution)/shard_map/ppermute | solution.py:432
  24.8 8.0 %collective-permute-start.7 = (bf16[2,8,32,128]{3,2,1,0:T(8,128)(2,1)S(1)}, bf16[2,8,32,128]{3,2,1,0:T(8,128)(2,1)S(1)}, u32[]{:S(2)}, u32[]{:S(2)}) collective-permute-start(bf16[2,8,32,128]{3,2,1,0:T(8,128)(2,1)S(1)} %get-tuple-element.56), channel_id=1, source_target_pairs={{0,192},{64,128},{128,64},{192,0},{1,193},{65,129},{129,65},{193,1... | collective-permute-start | bytes 393224 | tf_op jit(solution)/shard_map/ppermute | solution.py:432
